TPU v7x, 32 devices: a whole 2x2x4 slice. The times are simulated.
32 devices in a mesh: grp: 2 (over x), lat: 16 (over z, y, core).
Axes of the slice: x: 2, y: 2, z: 4, core: 2. Of those that a mesh axis runs over, the one named last changes fastest.
Arguments:
- coarse: bfloat16 [80, 64, 512], P(None, ('grp', 'lat')), parts along dimension 1, may hold values from -6 to 6
- reg_gain: float32 [2, 80], replicated, may hold values from 0.25 to 1.75
- reg_weight: bfloat16 [2, 3, 3, 80, 80], replicated, may hold values from -0.21875 to 0.21875
- reg_bias: float32 [2, 80], replicated, may hold values from -1.5 to 1.5
- noisy: bfloat16 [32, 4, 32, 512], P(('grp', 'lat')), parts along dimension 0, may hold values from -6 to 6
- lift_weight: bfloat16 [3, 3, 192, 84], replicated, may hold values from -0.21875 to 0.21875
- lift_bias: float32 [192], replicated, may hold values from -1.5 to 1.5
- mid_gain: float32 [192], replicated, may hold values from 0.25 to 1.75
- mid_weight: bfloat16 [3, 3, 192, 192], replicated, may hold values from -0.15625 to 0.15625
- mid_bias: float32 [192], replicated, may hold values from -1.5 to 1.5
Outputs:
- fine_level: bfloat16 [32, 192, 32, 512], P(('grp', 'lat')), parts along dimension 0
There are 2 independent parts, one for each index of `grp`. A program takes and returns all parts, laid end to end along the dimension named above; an argument that names none is the same for every part. Nothing has to cross between parts.
All inputs are finite; a program needn't handle non-finite values.
Results may differ from a plain program's by a relative error of at most 0.007.
Values may be sent and summed in bfloat16 or wider, within the bound.
A program may use at most 320 MiB of HBM per device.

v0:
```python
import functools

import jax
import jax.numpy as jnp
from jax import lax
from jax.experimental import pallas as pl
from jax.experimental.pallas import tpu as pltpu
from jax.sharding import PartitionSpec as P

TILE_COLS = 4
LAT_UP = 4
LON_UP = 4
EPSILON = 1e-06
F32 = jnp.float32
BF16 = jnp.bfloat16
MESH = pl.DeviceIdType.MESH
HALF = 64


def activate(values, half_gain):
    inverse = lax.rsqrt(jnp.mean(values * values, axis=0, keepdims=True) + EPSILON)
    half = values * inverse * half_gain
    return half + half * jnp.tanh(half)


def split(numerator, factor):
    lower = numerator // (2 * factor)
    return lower, (numerator - 2 * factor * lower).astype(F32) / (2.0 * factor)


def column(row):
    n = row.shape[1]
    here = lax.broadcasted_iota(jnp.int32, (n, n), 0) == lax.broadcasted_iota(jnp.int32, (n, n), 1)
    return jnp.broadcast_to(jnp.sum(jnp.where(here, row, 0.0), axis=1, keepdims=True), (n, 128))


def nt_dot(a, b):
    return lax.dot_general(a, b, (((1,), (1,)), ((), ())), preferred_element_type=F32)


def first_kernel(
    coarse, noisy, gain, regb, regs, lifts, mids,
    field, ring, got_rows, liftw, midw, lon,
    band, pieces, got, tile, cols, rows, got_cols, far_rows, regv, liftv, midv, regw, liftt, held, part,
    send, recv, nsend, nrecv, local,
):
    me = lax.axis_index("lat")
    tile_rows = lax.axis_size("lat") // TILE_COLS
    r = me // TILE_COLS
    c = me % TILE_COLS
    north, south = r > 0, r < tile_rows - 1
    top, bottom = r == 0, r == tile_rows - 1
    cin, band_rows, clon = band.shape
    ch = midv.shape[1]
    nout, fr, fl = tile.shape
    blocks = regw.shape[0]
    halo = blocks + 1
    span = 2 * halo * TILE_COLS
    cw = held.shape[2]
    lines_n = held.shape[0]
    spare = (lines_n - band_rows * TILE_COLS) // 2

    barrier = pltpu.get_barrier_semaphore()

    def greet(target):
        pl.semaphore_signal(barrier, inc=1, device_id={"lat": target}, device_id_type=MESH)

    for k in range(1, TILE_COLS):
        greet(r * TILE_COLS + (c + k) % TILE_COLS)

    @pl.when(north)
    def _():
        for k in range(TILE_COLS):
            greet((r - 1) * TILE_COLS + k)

    @pl.when(south)
    def _():
        for k in range(TILE_COLS):
            greet((r + 1) * TILE_COLS + k)

    loads = [
        pltpu.make_async_copy(coarse, band, local.at[0]),
        pltpu.make_async_copy(noisy.at[0], tile, local.at[1]),
        pltpu.make_async_copy(regs, regv, local.at[2]),
        pltpu.make_async_copy(mids, midv, local.at[3]),
        pltpu.make_async_copy(lifts, liftv, local.at[4]),
    ]
    for load in loads:
        load.start()

    lane = lax.broadcasted_iota(jnp.int32, (1, 128), 1)
    loads[0].wait()
    for sub in range(band_rows):
        row = band[:, sub, :].astype(F32)
        parts = [row[:, b * 128:(b + 1) * 128] for b in range(TILE_COLS)]
        for b in range(TILE_COLS):
            pieces[b, sub, :cin, :] = parts[b].astype(BF16)
        side = jnp.zeros((16, 128), F32)
        for b in range(TILE_COLS):
            seam = jnp.where(lane < 64, parts[b], parts[(b + TILE_COLS - 1) % TILE_COLS])
            for g in range(cin // 16):
                at = g * span + 2 * halo * b
                moved = pltpu.roll(seam[g * 16:(g + 1) * 16], at + halo, 1)
                side = jnp.where(jnp.logical_and(lane >= at, lane < at + 2 * halo), moved, side)
        for b in range(TILE_COLS):
            pieces[b, sub, cin:, :] = side.astype(BF16)

    loads[1].wait()
    ends = []
    for n in range(nout):
        ends += [tile[n, :2, :].astype(F32), tile[n, fr - 2:, :].astype(F32)]
    rows[...] = jnp.concatenate(ends, axis=0).astype(BF16)
    pick_row = lax.broadcasted_iota(jnp.int32, (4 * nout, 128), 0)
    pick_lane = lax.broadcasted_iota(jnp.int32, (4 * nout, 128), 1)
    packed = jnp.zeros((4 * nout, fr), F32)
    for n in range(nout):
        for s, (lo, at) in enumerate(((0, 0), (0, 1), (fl - 128, 126), (fl - 128, 127))):
            if s % 2 == 0:
                hit = jnp.zeros(pick_row.shape, jnp.bool_)
            hit = jnp.logical_or(hit, jnp.logical_and(pick_row == s * nout + n, pick_lane == at))
            if s % 2:
                packed = packed + nt_dot(jnp.where(hit, 1.0, 0.0).astype(BF16), tile[n, :, lo:lo + 128])
    cols[...] = jnp.concatenate([packed, jnp.zeros((4 * nout, 128 - fr), F32)], axis=1).astype(BF16)

    peers = TILE_COLS - 1 + jnp.where(north, TILE_COLS, 0) + jnp.where(south, TILE_COLS, 0)
    pl.semaphore_wait(barrier, peers)

    def remote(src, dst, ssem, rsem, target):
        return pltpu.make_async_remote_copy(
            src_ref=src, dst_ref=dst, send_sem=ssem, recv_sem=rsem,
            device_id={"lat": target}, device_id_type=MESH)

    whole, upper, lower = (0, 2), (0, 1), (1, 1)

    def landing(slot, span_rows):
        return got.at[pl.ds(2 * slot + span_rows[0], span_rows[1])]

    def band_copy(k, row, slot, ssem, span_rows=whole):
        col = (c + k) % TILE_COLS
        return remote(pieces.at[col, pl.ds(*span_rows)], landing(slot, span_rows), send.at[ssem], recv.at[slot],
                      row * TILE_COLS + col)

    west, east = (c + TILE_COLS - 1) % TILE_COLS, (c + 1) % TILE_COLS

    def col_copy(slot, row, col):
        return remote(cols, got_cols.at[slot], nsend.at[slot], nrecv.at[slot], row * TILE_COLS + col)

    def row_copy(slot, row):
        return remote(rows, far_rows.at[slot], nsend.at[8 + slot], nrecv.at[8 + slot], row * TILE_COLS + c)

    def each_band(action):
        for col, side, row, slot, span_rows in (
            (2, south, r + 1, 0, lower), (3, south, r + 1, 1, whole),
            (0, north, r - 1, 6, whole), (1, north, r - 1, 7, upper),
        ):
            @pl.when(jnp.logical_and(side, c == col))
            def _():
                for k in range(TILE_COLS):
                    action(band_copy(k, row, slot, TILE_COLS + k, span_rows))

        for k in range(1, TILE_COLS):
            action(band_copy(k, r, 2 + c, k))

    def each_edge(action):
        action(col_copy(0, r, east))
        action(col_copy(1, r, west))

        @pl.when(south)
        def _():
            action(row_copy(0, r + 1))
            action(col_copy(6, r + 1, c))
            action(col_copy(2, r + 1, east))
            action(col_copy(3, r + 1, west))

        @pl.when(north)
        def _():
            action(row_copy(1, r - 1))
            action(col_copy(7, r - 1, c))
            action(col_copy(4, r - 1, east))
            action(col_copy(5, r - 1, west))

    each_band(lambda copy: copy.start())
    own = pltpu.make_async_copy(pieces.at[c], landing(2 + c, whole), local.at[5])
    own.start()

    loads[2].wait()
    for k in range(blocks):
        for p in range(3):
            for q in range(3):
                regw[k, p * cin:(p + 1) * cin, q * cin:(q + 1) * cin] = regv[9 * k + 3 * p + q]
    each_edge(lambda copy: copy.start())

    loads[3].wait()
    for tap in range(9):
        midw[:, tap * ch:(tap + 1) * ch] = midv[tap]
    loads[4].wait()
    slab = liftt.shape[0] // 3
    for p in range(3):
        noise = []
        for q in range(3):
            base = p * slab + q * cin
            liftt[base:base + cin, :] = liftv[3 * p + q, :cin, :]
            noise.append(liftv[3 * p + q, cin:, :].astype(F32))
        noise.append(jnp.zeros((slab - 3 * (cin + nout), ch), F32))
        liftt[p * slab + 3 * cin:(p + 1) * slab, :] = jnp.concatenate(noise, axis=0).astype(BF16)
    eye = jnp.where(lax.broadcasted_iota(jnp.int32, (ch, ch), 0) == lax.broadcasted_iota(jnp.int32, (ch, ch), 1), 1.0, 0.0)
    liftw[...] = nt_dot(eye.astype(BF16), liftt[...]).astype(BF16)

    position = lax.broadcasted_iota(jnp.int32, (1, 3 * fl), 1)
    shift = jnp.where(position >= 2 * fl, 2, jnp.where(position >= fl, 1, 0))
    low, weight = lon_split(position - shift * fl + shift - 1)
    low_lane = jnp.where(low < 0, low + cw, low)
    high_lane = jnp.where(low + 1 < 0, low + 1 + cw, low + 1)
    coarse_lane = lax.broadcasted_iota(jnp.int32, (cw, 3 * fl), 0)
    lon[...] = jnp.where(coarse_lane == low_lane, 1.0 - weight,
                         jnp.where(coarse_lane == high_lane, weight, 0.0)).astype(BF16)

    own.wait()

    def arrived(slot, span_rows=whole):
        remote(pieces.at[0, pl.ds(*span_rows)], landing(slot, span_rows), send.at[0], recv.at[slot], me).wait_recv()

    def edge(slot):
        if slot < 8:
            remote(cols, got_cols.at[slot], nsend.at[slot], nrecv.at[slot], me).wait_recv()
        else:
            remote(rows, far_rows.at[slot - 8], nsend.at[slot], nrecv.at[slot], me).wait_recv()

    for k in range(1, TILE_COLS):
        arrived(2 + (c + k) % TILE_COLS)

    @pl.when(north)
    def _():
        arrived(0, lower)
        arrived(1)

    @pl.when(south)
    def _():
        arrived(6)
        arrived(7, upper)

    def real(i):
        row = r * (lines_n - 2 * spare) - spare + i
        return jnp.logical_and(row >= 0, row < (lines_n - 2 * spare) * tile_rows)

    half_gains = [column(gain[k:k + 1, :])[:, :1] * 0.5 for k in range(blocks)]
    biases = [column(regb[k:k + 1, :])[:, :1] for k in range(blocks)]

    def spread(k, i, values):
        values = activate(values, half_gains[k])
        taps = jnp.concatenate(
            [pltpu.roll(values, 1, 1).astype(BF16), values.astype(BF16), pltpu.roll(values, cw - 1, 1).astype(BF16)],
            axis=0)
        part[k % 2, i] = jnp.dot(regw[k], taps, preferred_element_type=F32)

    def enter(i, _):
        own_cols = got[i, :cin, :].astype(F32)
        side = got[i, cin:, :].astype(F32)
        outer = []
        for g in range(cin // 16):
            after = pltpu.roll(side, 128 - halo - g * span - 2 * halo * east, 1)
            before = pltpu.roll(side, 128 - halo - g * span - 2 * halo * c, 1)
            outer.append(jnp.where(lane < halo, after, jnp.where(lane >= 128 - halo, before, 0.0)))
        values = jnp.concatenate([own_cols, jnp.concatenate(outer, axis=0)], axis=1)
        values = jnp.where(real(i), values, 0.0)
        held[i] = values
        spread(0, i, values)
        return 0

    lax.fori_loop(1, lines_n - 1, enter, 0, unroll=2)

    def update(k, i):
        values = held[i] + part[k % 2, i - 1, :cin, :] + part[k % 2, i, cin:2 * cin, :] + part[k % 2, i + 1, 2 * cin:, :]
        values = (values + biases[k]).astype(BF16)
        return jnp.where(real(i), values.astype(F32), 0.0)

    for k in range(1, blocks):
        def follow(i, _, k=k):
            values = update(k - 1, i)
            held[i] = values
            spread(k, i, values)
            return 0

        lax.fori_loop(1 + k, lines_n - 1 - k, follow, 0, unroll=2)

    def leave(i, _):
        field[i - halo] = update(blocks - 1, i).astype(BF16)
        return 0

    lax.fori_loop(halo, lines_n - halo, leave, 0, unroll=2)

    edge(0)
    edge(1)

    @pl.when(north)
    def _():
        for slot in (2, 3, 6, 8):
            edge(slot)

    @pl.when(south)
    def _():
        for slot in (4, 5, 7, 9):
            edge(slot)

    def along(middle, above, below):
        above = jnp.where(top, 0.0, pltpu.roll(above.astype(F32), 128 - (fr - 2), 1))
        below = jnp.where(bottom, 0.0, pltpu.roll(below.astype(F32), fr + 2, 1))
        middle = pltpu.roll(middle.astype(F32), 2, 1)
        return jnp.where(lane < 2, above, jnp.where(lane < fr + 2, middle, below))

    ring[0] = along(got_cols[0], got_cols[2], got_cols[4])
    ring[1] = along(got_cols[1], got_cols[3], got_cols[5])
    ring[2] = along(cols[...], got_cols[6], got_cols[7])
    got_rows[...] = far_rows[...]
    each_band(lambda copy: copy.wait_send())
    each_edge(lambda copy: copy.wait_send())


def lon_split(fine_col):
    lower, part = split(2 * fine_col + 1 - LON_UP + 2 * LON_UP, LON_UP)
    return lower - 1, part


def first_program(coarse, noisy, gain, regb, regs, lifts, mids):
    any_space = pl.BlockSpec(memory_space=pl.ANY)
    vmem = pl.BlockSpec(memory_space=pltpu.VMEM)
    dma = pltpu.SemaphoreType.DMA
    cin, band_rows, clon = coarse.shape
    nout, fr, fl = noisy.shape[1:]
    ch = mids.shape[1]
    blocks = regs.shape[0] // 9
    slab = 3 * cin + -(-3 * nout // 16) * 16
    lines_n = band_rows * (TILE_COLS + 4)
    count = lines_n - 2 * (blocks + 1)
    ct_lon = clon // TILE_COLS
    cw = 2 * ct_lon
    assert ct_lon == 128 and cin % 16 == 0 and band_rows == 2
    assert (cin // 16) * 2 * (blocks + 1) * TILE_COLS <= 128
    shape = jax.ShapeDtypeStruct
    return pl.pallas_call(
        first_kernel,
        out_shape=(
            shape((count, cin, cw), BF16),
            shape((3, 4 * nout, 128), F32),
            shape((2, 4 * nout, fl), BF16),
            shape((ch, 3 * slab), BF16),
            shape((ch, 9 * ch), BF16),
            shape((cw, 3 * fl), BF16),
        ),
        in_specs=[any_space] * 2 + [vmem] * 2 + [any_space] * 3,
        out_specs=(vmem,) * 6,
        scratch_shapes=[
            pltpu.VMEM((cin, band_rows, clon), BF16),
            pltpu.VMEM((TILE_COLS, band_rows, cin + 16, 128), BF16),
            pltpu.VMEM((lines_n, cin + 16, 128), BF16),
            pltpu.VMEM((nout, fr, fl), BF16),
            pltpu.VMEM((4 * nout, 128), BF16),
            pltpu.VMEM((4 * nout, fl), BF16),
            pltpu.VMEM((8, 4 * nout, 128), BF16),
            pltpu.VMEM((2, 4 * nout, fl), BF16),
            pltpu.VMEM(regs.shape, BF16),
            pltpu.VMEM(lifts.shape, BF16),
            pltpu.VMEM(mids.shape, BF16),
            pltpu.VMEM((blocks, 3 * cin, 3 * cin), BF16),
            pltpu.VMEM((3 * slab, ch), BF16),
            pltpu.VMEM((lines_n, cin, cw), F32),
            pltpu.VMEM((2, lines_n, 3 * cin, cw), F32),
            dma((2 * TILE_COLS,)), dma((8,)), dma((10,)), dma((10,)), dma((6,)),
        ],
        compiler_params=pltpu.CompilerParams(
            collective_id=0, has_side_effects=True, vmem_limit_bytes=24_000_000),
    )(coarse, noisy, gain, regb, regs, lifts, mids)


def tile_kernel(
    dims, field, tile, ring, got_rows, liftw, liftb, midg, midw, midb, lon, out,
    grid, lines, upper, sides, bands, keep, raw, prod, edges, cols, rows_out, stage, sems,
):
    cin, ch, fr, fl = dims
    count, cw = field.shape[0], field.shape[2]
    tile_row, tile_rows = lax.axis_index("lat") // TILE_COLS, lax.axis_size("lat") // TILE_COLS
    nout = tile.shape[1]
    top, bottom = tile_row == 0, tile_row == tile_rows - 1
    steps = bands.shape[0]
    wide = fl // 128

    cols[0] = column(liftb[...])
    cols[1] = column(midg[...]) * 0.5
    cols[2] = column(midb[...])

    for q in range(3):
        lines[:, q * cin:(q + 1) * cin, :] = jnp.dot(
            field[...].reshape(count * cin, cw), lon[:, q * fl:(q + 1) * fl],
            preferred_element_type=F32).reshape(count, cin, fl)

    low_line = jnp.where(top, 1, 0)
    high_line = jnp.where(bottom, count - 2, count - 1)
    fine_total = fr * tile_rows

    def inside(t):
        row = tile_row * fr + t - 2
        return jnp.logical_and(row >= 0, row < fine_total)

    def lat_split(t):
        lower, part = split(2 * (t - 2) + 1 - LAT_UP + 2 * LAT_UP, LAT_UP)
        return jnp.clip(lower, low_line, high_line), jnp.clip(lower + 1, low_line, high_line), part

    slab = upper.shape[1]
    lane = lax.broadcasted_iota(jnp.int32, (1, 128), 1)
    lane_first, lane_last = lane == 0, lane == 127

    tall = fr + 4
    for n in range(nout):
        for j in range(wide):
            at = slice(j * 128, (j + 1) * 128)
            base = n * tall
            grid[j, base + 2:base + 2 + fr, :] = tile[0, n, :, at].astype(F32)
            above = got_rows[0, :, at].astype(F32)[4 * n + 2:4 * n + 4]
            below = got_rows[1, :, at].astype(F32)[4 * n:4 * n + 2]
            grid[j, base:base + 2, :] = jnp.where(top, 0.0, above)
            grid[j, base + 2 + fr:base + tall, :] = jnp.where(bottom, 0.0, below)

    west, east, here = ring[0], ring[1], ring[2]
    none = jnp.zeros((slab - 3 * (cin + nout), 128), F32)
    left_cols = jnp.concatenate([west[2 * nout:], here[:nout], none], axis=0)
    right_cols = jnp.concatenate([here[3 * nout:], east[:2 * nout], none], axis=0)
    west_col, east_col = west[3 * nout:], east[:nout]

    def noise_rows(t):
        rows = [grid[j, pl.ds(t, nout, stride=tall), :] for j in range(wide)]
        onward = [pltpu.roll(v, 1, 1) for v in rows]
        back = [pltpu.roll(v, 127, 1) for v in rows]
        edge_l = pltpu.roll(west_col, (128 - t) % 128 if isinstance(t, int) else 128 - t, 1)
        edge_r = pltpu.roll(east_col, 127 - t, 1)
        pieces = []
        for j in range(wide):
            lo = jnp.where(lane_first, onward[j - 1] if j else edge_l, onward[j])
            hi = jnp.where(lane_last, back[j + 1] if j < wide - 1 else edge_r, back[j])
            pieces.append(jnp.concatenate([lo, rows[j], hi, none], axis=0))
        return jnp.concatenate(pieces, axis=1).astype(BF16)

    def raise_row(t, slot):
        a, b, part = lat_split(jnp.int32(t))
        ok = inside(t)
        wa = jnp.where(ok, 1.0 - part, 0.0)
        wb = jnp.where(ok, part, 0.0)
        for o in range(0, 3 * cin, 16):
            upper[slot, o:o + 16, :] = (wa * lines[a, o:o + 16, :] + wb * lines[b, o:o + 16, :]).astype(BF16)
        upper[slot, 3 * cin:slab, :] = noise_rows(t)

    edge_row = jnp.where(lane < HALF, lane, lane - HALF)
    near = fl // LON_UP
    picked_cols = [-1, 0, near - 1, near]
    select_lane = lax.broadcasted_iota(jnp.int32, (cw, 128), 0)
    select_pos = lax.broadcasted_iota(jnp.int32, (cw, 128), 1)
    hits = jnp.zeros((cw, 128), jnp.bool_)
    for s, col in enumerate(picked_cols):
        hits = jnp.logical_or(hits, jnp.logical_and(select_pos == s, select_lane == col % cw))
    chosen = jnp.where(hits, 1.0, 0.0).astype(BF16)
    packed = jnp.zeros((cin, 128), F32)
    for i in range(count):
        narrow = jnp.dot(field[i], chosen, preferred_element_type=F32)
        packed = packed + (pltpu.roll(narrow, 4 * i, 1) if i else narrow)
    packed = packed.astype(BF16)
    key = lax.broadcasted_iota(jnp.int32, (128, 1), 0)
    key_line = key // 4
    key_pick = key - 4 * key_line
    key_col = jnp.where(key_pick == 0, picked_cols[0], jnp.where(
        key_pick == 1, picked_cols[1], jnp.where(key_pick == 2, picked_cols[2], picked_cols[3])))
    for p in range(3):
        t = edge_row + p
        a, b, part = lat_split(t)
        ok = inside(t)
        wa = jnp.where(ok, 1.0 - part, 0.0)
        wb = jnp.where(ok, part, 0.0)
        by_row = jnp.where(key_line == a, wa, 0.0) + jnp.where(key_line == b, wb, 0.0)
        for q in range(3):
            lower, part_m = lon_split(jnp.where(lane < HALF, q - 2, fl - 1 + q))
            by_col = jnp.where(key_col == lower, 1.0 - part_m, jnp.where(key_col == lower + 1, part_m, 0.0))
            base = p * slab + q * cin
            sides[base:base + cin, :] = jnp.dot(
                packed, (by_row * by_col).astype(BF16), preferred_element_type=F32).astype(BF16)
        sides[p * slab + 3 * cin:(p + 1) * slab, :] = jnp.where(
            lane < HALF, pltpu.roll(left_cols, (128 - p) % 128, 1), pltpu.roll(right_cols, HALF - p, 1)).astype(BF16)
    edge_lift = jnp.dot(liftw[...], sides[...], preferred_element_type=F32) + cols[0]
    edge_lift = edge_lift.astype(BF16).astype(F32)
    edges[...] = jnp.where(inside(edge_row + 1), activate(edge_lift, cols[1]), 0.0)

    def lift(slot):
        window = jnp.concatenate([upper[(slot + n) % steps] for n in range(3)], axis=0)
        raw[slot % 2] = jnp.dot(liftw[...], window, preferred_element_type=F32)

    def finish(l, slot):
        squares = jnp.zeros((8, fl), F32)
        for o in range(0, ch, 16):
            bias = jnp.concatenate([cols[0, o:o + 16, :]] * wide, axis=1)
            rounded = (raw[slot % 2, o:o + 16, :] + bias).astype(BF16)
            keep[slot, o:o + 16, :] = rounded
            values = rounded.astype(F32)
            values = values * values
            squares = squares + (values[:8] + values[8:])
        inverse = lax.rsqrt(jnp.sum(squares, axis=0, keepdims=True) * (1.0 / ch) + EPSILON)
        inverse = jnp.where(inside(l + 1), inverse, 0.0)
        for o in range(0, ch, 16):
            half_gain = jnp.concatenate([cols[1, o:o + 16, :]] * wide, axis=1)
            half = keep[slot, o:o + 16, :].astype(F32) * inverse * half_gain
            values = half + half * jnp.tanh(half)
            edge = edges[o:o + 16, :]
            parts = [values[:, j * 128:(j + 1) * 128] for j in range(wide)]
            east = [pltpu.roll(v, 1, 1) for v in parts]
            west = [pltpu.roll(v, 127, 1) for v in parts]
            edge_l = pltpu.roll(edge, 128 - l, 1)
            edge_r = pltpu.roll(edge, 128 + HALF - 1 - l, 1)
            bands[slot, ch + o:ch + o + 16, :] = values.astype(BF16)
            bands[slot, o:o + 16, :] = jnp.concatenate(
                [jnp.where(lane_first, east[j - 1] if j else edge_l, east[j]) for j in range(wide)],
                axis=1).astype(BF16)
            bands[slot, 2 * ch + o:2 * ch + o + 16, :] = jnp.concatenate(
                [jnp.where(lane_last, west[j + 1] if j < wide - 1 else edge_r, west[j]) for j in range(wide)],
                axis=1).astype(BF16)

    def mid(slot):
        window = jnp.concatenate([bands[(slot + n) % steps] for n in range(3)], axis=0)
        prod[slot % 2] = jnp.dot(midw[...], window, preferred_element_type=F32)

    group = stage.shape[2]

    def flush(part):
        slot = part % 2

        def copy(n):
            return pltpu.make_async_copy(
                stage.at[n % 2], out.at[0, :, pl.ds(pl.multiple_of(n * group, group), group), :], sems.at[n % 2])

        @pl.when(part >= 2)
        def _():
            copy(part - 2).wait()

        def shrink(o, _):
            for j in range(wide):
                block = rows_out[j, pl.ds(pl.multiple_of(o * 8 * group, 8 * group), 8 * group), :]
                stage[slot, pl.ds(o * 8, 8), :, j * 128:(j + 1) * 128] = block.reshape(8, group, 128).astype(BF16)
            return 0

        lax.fori_loop(0, ch // 8, shrink, 0)
        copy(part).start()

    def emit(y, slot):
        spot = y % group
        for o in range(0, ch, 16):
            bias = cols[2, o:o + 16, :]
            for j in range(wide):
                at = slice(j * 128, (j + 1) * 128)
                total = keep[(slot + 1) % steps, o:o + 16, at].astype(F32) + prod[slot % 2, o:o + 16, at] + bias
                rows_out[j, pl.ds(spot + o * group, 16, stride=group), :] = total

    for t in range(3):
        raise_row(t, t % steps)
    for l in range(3):
        lift(l % steps)
        raise_row(l + 3, (l + 3) % steps)
        finish(jnp.int32(l), l % steps)

    def trip(i, _):
        for j in range(steps):
            l = i * steps + j + 3
            slot = (j + 3) % steps
            lift(slot)
            mid(j)
            raise_row(jnp.minimum(l + 3, fr + 3), (j + 6) % steps)
            finish(l, slot)
            emit(l - 3, j)

        @pl.when((i + 1) % (group // steps) == 0)
        def _():
            flush(i // (group // steps))
        return 0

    lax.fori_loop(0, fr // steps, trip, 0)
    parts = fr // group
    for n in range(max(parts - 2, 0), parts):
        pltpu.make_async_copy(stage.at[n % 2], out.at[0, :, pl.ds(n * group, group), :], sems.at[n % 2]).wait()


def tile_program(field, noisy, ring, got_rows, liftw, liftb, midg, midw, midb, lon):
    count, cin, cw = field.shape
    ch = liftw.shape[0]
    nout, fr, fl = noisy.shape[1:]
    group = 16
    steps = 4
    vmem = pl.BlockSpec(memory_space=pltpu.VMEM)
    slab = liftw.shape[1] // 3
    return pl.pallas_call(
        functools.partial(tile_kernel, (cin, ch, fr, fl)),
        out_shape=jax.ShapeDtypeStruct((1, ch, fr, fl), BF16),
        in_specs=[vmem] * 10,
        out_specs=pl.BlockSpec(memory_space=pl.ANY),
        scratch_shapes=[
            pltpu.VMEM((fl // 128, nout * (fr + 4), 128), F32),
            pltpu.VMEM((count, 3 * cin, fl), F32),
            pltpu.VMEM((steps, slab, fl), BF16),
            pltpu.VMEM((3 * slab, 128), BF16),
            pltpu.VMEM((steps, 3 * ch, fl), BF16),
            pltpu.VMEM((steps, ch, fl), BF16),
            pltpu.VMEM((2, ch, fl), F32),
            pltpu.VMEM((2, ch, fl), F32),
            pltpu.VMEM((ch, 128), F32),
            pltpu.VMEM((3, ch, 128), F32),
            pltpu.VMEM((fl // 128, ch * group, 128), F32),
            pltpu.VMEM((2, ch, group, fl), BF16),
            pltpu.SemaphoreType.DMA((2,)),
        ],
        compiler_params=pltpu.CompilerParams(vmem_limit_bytes=40_000_000),
    )(field, noisy, ring, got_rows, liftw, liftb, midg, midw, midb, lon)


def per_device(
    coarse, reg_gain, reg_weight, reg_bias, noisy, lift_weight, lift_bias, mid_gain, mid_weight, mid_bias,
):
    lifts = lift_weight.transpose(0, 1, 3, 2)
    field, ring, got_rows, liftw, midw, lon = first_program(
        coarse, noisy, reg_gain, reg_bias, reg_weight.reshape((-1,) + reg_weight.shape[3:]),
        lifts.reshape((9,) + lifts.shape[2:]), mid_weight.reshape((9,) + mid_weight.shape[2:]))
    return tile_program(
        field, noisy, ring, got_rows, liftw, lift_bias[None], mid_gain[None], midw, mid_bias[None], lon)


def solution(mesh):
    placed = (
        P(None, ("grp", "lat"), None),
        P(),
        P(),
        P(),
        P(("grp", "lat"), None, None, None),
        P(),
        P(),
        P(),
        P(),
        P(),
    )
    return jax.shard_map(
        per_device,
        mesh=mesh,
        in_specs=placed,
        out_specs=P(("grp", "lat"), None, None, None),
        check_vma=False,
    )
```

profile of v0, /device:TPU:0, one launch (start us, length us, event | category | flops | bytes accessed | tf_op | source)
XLA Modules:
  0.0 56.0 jit_solution(6138015958490953642)
XLA Ops:
  0.0 0.0 copy-start
  0.0 1.2 %copy-done = bf16[3,3,192,192]{3,2,1,0:T(8,128)(2,1)S(1)} copy-done((bf16[3,3,192,192]{3,2,1,0:T(8,128)(2,1)S(1)}, bf16[3,3,192,192]{3,2,1,0:T(8,128)(2,1)}, u32[]{:S(2)}) %copy-start) | copy-done | bytes 663576
  1.2 0.0 copy-start.1
  1.2 0.9 %copy-done.1 = bf16[1,4,32,512]{3,2,1,0:T(8,128)(2,1)S(1)} copy-done((bf16[1,4,32,512]{3,2,1,0:T(8,128)(2,1)S(1)}, bf16[1,4,32,512]{3,2,1,0:T(8,128)(2,1)}, u32[]{:S(2)}) %copy-start.1) | copy-done | bytes 131096
  2.1 0.0 copy-start.3
  2.1 1.0 %copy-done.3 = bf16[3,3,192,84]{2,3,1,0:T(8,128)(2,1)S(1)} copy-done((bf16[3,3,192,84]{2,3,1,0:T(8,128)(2,1)S(1)}, bf16[3,3,192,84]{2,3,1,0:T(8,128)(2,1)}, u32[]{:S(2)}) %copy-start.3) | copy-done | bytes 290328
  3.1 0.0 copy-start.4
  3.1 1.0 %copy-done.4 = bf16[2,3,3,80,80]{4,3,2,1,0:T(8,128)(2,1)S(1)} copy-done((bf16[2,3,3,80,80]{4,3,2,1,0:T(8,128)(2,1)S(1)}, bf16[2,3,3,80,80]{4,3,2,1,0:T(8,128)(2,1)}, u32[]{:S(2)}) %copy-start.4) | copy-done | bytes 230424
  4.1 0.0 copy-start.5
  4.1 0.9 %copy-done.5 = bf16[80,2,512]{2,1,0:T(2,128)(2,1)S(1)} copy-done((bf16[80,2,512]{2,1,0:T(2,128)(2,1)S(1)}, bf16[80,2,512]{2,1,0:T(2,128)(2,1)}, u32[]{:S(2)}) %copy-start.5) | copy-done | bytes 163864
  5.0 0.0 copy-start.6
  5.0 0.7 %copy-done.6 = f32[2,80]{1,0:T(2,128)S(1)} copy-done((f32[2,80]{1,0:T(2,128)S(1)}, f32[2,80]{1,0:T(2,128)}, u32[]{:S(2)}) %copy-start.6) | copy-done | bytes 664
  5.7 0.0 copy-start.7
  5.7 0.7 %copy-done.7 = f32[2,80]{1,0:T(2,128)S(1)} copy-done((f32[2,80]{1,0:T(2,128)S(1)}, f32[2,80]{1,0:T(2,128)}, u32[]{:S(2)}) %copy-start.7) | copy-done | bytes 664
  6.3 16.1 %shard_map.100 = (bf16[10,80,256]{2,1,0:T(8,128)(2,1)S(1)}, f32[3,16,128]{2,1,0:T(8,128)S(1)}, bf16[2,16,512]{2,1,0:T(8,128)(2,1)S(1)}, bf16[192,768]{1,0:T(8,12...) custom-call(bf16[80,2,512]{2,1,0:T(2,128)(2,1)S(1)} %copy-done.5, ...), custom_call_target="tpu_custom_call" | custom-call | tf_op jit(solution)/shard_map/pallas_call | solution.py:340
  22.4 0.0 copy-start.2
  22.4 0.9 %copy-done.2 = bf16[1,4,32,512]{3,2,1,0:T(8,128)(2,1)S(1)} copy-done((bf16[1,4,32,512]{3,2,1,0:T(8,128)(2,1)S(1)}, bf16[1,4,32,512]{3,2,1,0:T(8,128)(2,1)}, u32[]{:S(2)}) %copy-start.2) | copy-done | bytes 131096
  23.3 0.0 copy-start.8
  23.3 0.7 %copy-done.8 = f32[192]{0:T(256)S(1)} copy-done((f32[192]{0:T(256)S(1)}, f32[192]{0:T(256)}, u32[]{:S(2)}) %copy-start.8) | copy-done | bytes 792
  24.0 0.0 copy-start.9
  24.0 0.7 %copy-done.9 = f32[192]{0:T(256)S(1)} copy-done((f32[192]{0:T(256)S(1)}, f32[192]{0:T(256)}, u32[]{:S(2)}) %copy-start.9) | copy-done | bytes 792
  24.7 0.0 copy-start.10
  24.7 0.7 %copy-done.10 = f32[192]{0:T(256)S(1)} copy-done((f32[192]{0:T(256)S(1)}, f32[192]{0:T(256)}, u32[]{:S(2)}) %copy-start.10) | copy-done | bytes 792
  25.3 30.7 %shard_map.101 = bf16[1,192,32,512]{3,2,1,0:T(8,128)(2,1)} custom-call(bf16[10,80,256]{2,1,0:T(8,128)(2,1)S(1)} %get-tuple-element.11.field, bf16[1,4,32,512]{3,2,1,0:T(8,128)(2,1)S(1)} %copy-done.2, f32[3,16,128]{2,1,0:T(8,128)S(1)} %get-tuple-element.12.ring, bf16[2,16,512]{2,1,0:T(8,128)(2,1)S(1)} %get-tuple-element.13.got_rows, ...), custom_call_target="tpu_custom_call" | custom-call | tf_op jit(solution)/shard_map/pallas_call | solution.py:593
Async XLA Ops:
  0.0 1.2 %copy-start = (bf16[3,3,192,192]{3,2,1,0:T(8,128)(2,1)S(1)}, bf16[3,3,192,192]{3,2,1,0:T(8,128)(2,1)}, u32[]{:S(2)}) copy-start(bf16[3,3,192,192]{3,2,1,0:T(8,128)(2,1)} %param.18) | copy-start | bytes 1990660
  1.2 0.9 %copy-start.1 = (bf16[1,4,32,512]{3,2,1,0:T(8,128)(2,1)S(1)}, bf16[1,4,32,512]{3,2,1,0:T(8,128)(2,1)}, u32[]{:S(2)}) copy-start(bf16[1,4,32,512]{3,2,1,0:T(8,128)(2,1)} %tile.1) | copy-start | bytes 393220
  2.1 1.0 %copy-start.3 = (bf16[3,3,192,84]{2,3,1,0:T(8,128)(2,1)S(1)}, bf16[3,3,192,84]{2,3,1,0:T(8,128)(2,1)}, u32[]{:S(2)}) copy-start(bf16[3,3,192,84]{2,3,1,0:T(8,128)(2,1)} %param.15) | copy-start | bytes 870916
  3.1 1.0 %copy-start.4 = (bf16[2,3,3,80,80]{4,3,2,1,0:T(8,128)(2,1)S(1)}, bf16[2,3,3,80,80]{4,3,2,1,0:T(8,128)(2,1)}, u32[]{:S(2)}) copy-start(bf16[2,3,3,80,80]{4,3,2,1,0:T(8,128)(2,1)} %param.12) | copy-start | bytes 691204
  4.1 0.9 %copy-start.5 = (bf16[80,2,512]{2,1,0:T(2,128)(2,1)S(1)}, bf16[80,2,512]{2,1,0:T(2,128)(2,1)}, u32[]{:S(2)}) copy-start(bf16[80,2,512]{2,1,0:T(2,128)(2,1)} %coarse.1) | copy-start | bytes 491524
  5.0 0.7 %copy-start.6 = (f32[2,80]{1,0:T(2,128)S(1)}, f32[2,80]{1,0:T(2,128)}, u32[]{:S(2)}) copy-start(f32[2,80]{1,0:T(2,128)} %gain.1) | copy-start | bytes 1924
  5.7 0.7 %copy-start.7 = (f32[2,80]{1,0:T(2,128)S(1)}, f32[2,80]{1,0:T(2,128)}, u32[]{:S(2)}) copy-start(f32[2,80]{1,0:T(2,128)} %regb.1) | copy-start | bytes 1924
  22.4 0.9 %copy-start.2 = (bf16[1,4,32,512]{3,2,1,0:T(8,128)(2,1)S(1)}, bf16[1,4,32,512]{3,2,1,0:T(8,128)(2,1)}, u32[]{:S(2)}) copy-start(bf16[1,4,32,512]{3,2,1,0:T(8,128)(2,1)} %tile.1) | copy-start | bytes 393220
  23.3 0.7 %copy-start.8 = (f32[192]{0:T(256)S(1)}, f32[192]{0:T(256)}, u32[]{:S(2)}) copy-start(f32[192]{0:T(256)} %param.16) | copy-start | bytes 2308
  24.0 0.7 %copy-start.9 = (f32[192]{0:T(256)S(1)}, f32[192]{0:T(256)}, u32[]{:S(2)}) copy-start(f32[192]{0:T(256)} %param.17) | copy-start | bytes 2308
  24.7 0.7 %copy-start.10 = (f32[192]{0:T(256)S(1)}, f32[192]{0:T(256)}, u32[]{:S(2)}) copy-start(f32[192]{0:T(256)} %param.19) | copy-start | bytes 2308
where the time goes:
time: 56.7 us; the launch traced here: 56 us
  Pallas kernels  46.7 us (82%)
  local copies, waits for them, and re-layouts  9.26 us (16%)
    pallas_call x1, Pallas kernels, tile_program(): pl.pallas_call(functools.partial(tile_kernel, (cin, ch, fr, fl)), out_sha...  30.7 us
    pallas_call x1, Pallas kernels, first_program(): pl.pallas_call(first_kernel, out_shape=(shape((count, cin, cw), BF16), sh...  16.1 us
    unnamed x22, local copies, waits for them, and re-layouts  9.26 us

commit v1 on v0

--- a/solution.py
+++ b/solution.py
@@ -38,10 +38,24 @@
     return lax.dot_general(a, b, (((1,), (1,)), ((), ())), preferred_element_type=F32)
 
 
+def lon_split(fine_col):
+    lower, part = split(2 * fine_col + 1 - LON_UP + 2 * LON_UP, LON_UP)
+    return lower - 1, part
+
+
+def lat_split(t, top, bottom, count, start, total):
+    lower, part = split(2 * (t - 2) + 1 - LAT_UP + 2 * LAT_UP, LAT_UP)
+    low_line = jnp.where(top, 1, 0)
+    high_line = jnp.where(bottom, count - 2, count - 1)
+    row = start + t - 2
+    ok = jnp.logical_and(row >= 0, row < total)
+    return jnp.clip(lower, low_line, high_line), jnp.clip(lower + 1, low_line, high_line), part, ok
+
+
 def first_kernel(
-    coarse, noisy, gain, regb, regs, lifts, mids,
-    field, ring, got_rows, liftw, midw, lon,
-    band, pieces, got, tile, cols, rows, got_cols, far_rows, regv, liftv, midv, regw, liftt, held, part,
+    coarse, noisy, gain, regb, regs, liftb, midg, midb, lifts, mids,
+    got, got_cols, cols, grid, regw, regc, liftw, liftc, midw, lon, sidew, chosen,
+    band, pieces, tile, rows, far_rows, gainv, regbv, vecs, regv, liftv, midv, liftt,
     send, recv, nsend, nrecv, local,
 ):
     me = lax.axis_index("lat")
@@ -56,9 +70,8 @@
     blocks = regw.shape[0]
     halo = blocks + 1
     span = 2 * halo * TILE_COLS
-    cw = held.shape[2]
-    lines_n = held.shape[0]
-    spare = (lines_n - band_rows * TILE_COLS) // 2
+    cw = chosen.shape[0]
+    count = got.shape[0] - 2 * halo
 
     barrier = pltpu.get_barrier_semaphore()
 
@@ -84,14 +97,25 @@
         pltpu.make_async_copy(regs, regv, local.at[2]),
         pltpu.make_async_copy(mids, midv, local.at[3]),
         pltpu.make_async_copy(lifts, liftv, local.at[4]),
+        pltpu.make_async_copy(gain, gainv, local.at[6]),
+        pltpu.make_async_copy(regb, regbv, local.at[7]),
+        pltpu.make_async_copy(liftb, vecs.at[0], local.at[8]),
+        pltpu.make_async_copy(midg, vecs.at[1], local.at[9]),
+        pltpu.make_async_copy(midb, vecs.at[2], local.at[10]),
     ]
     for load in loads:
         load.start()
 
     lane = lax.broadcasted_iota(jnp.int32, (1, 128), 1)
+    both = band_rows * cin
+    row_id = lax.broadcasted_iota(jnp.int32, (both, both), 0)
+    sub_id = jnp.where(row_id >= cin, 1, 0)
+    order = lax.broadcasted_iota(jnp.int32, (both, both), 1) == band_rows * (row_id - sub_id * cin) + sub_id
+    order = jnp.where(order, 1.0, 0.0).astype(BF16)
     loads[0].wait()
+    sorted_rows = jnp.dot(order, band[...].reshape(both, clon), preferred_element_type=F32)
     for sub in range(band_rows):
-        row = band[:, sub, :].astype(F32)
+        row = sorted_rows[sub * cin:(sub + 1) * cin]
         parts = [row[:, b * 128:(b + 1) * 128] for b in range(TILE_COLS)]
         for b in range(TILE_COLS):
             pieces[b, sub, :cin, :] = parts[b].astype(BF16)
@@ -215,6 +239,45 @@
     lon[...] = jnp.where(coarse_lane == low_lane, 1.0 - weight,
                          jnp.where(coarse_lane == high_lane, weight, 0.0)).astype(BF16)
 
+    for load in loads[5:]:
+        load.wait()
+    for k in range(blocks):
+        regc[2 * k] = column(gainv[k:k + 1, :]) * 0.5
+        regc[2 * k + 1] = column(regbv[k:k + 1, :])
+    liftc[0] = column(vecs[0])
+    liftc[1] = column(vecs[1]) * 0.5
+    liftc[2] = column(vecs[2])
+
+    tall = fr + 4
+    wide = fl // 128
+    for n in range(nout):
+        for j in range(wide):
+            grid[j, n * tall + 2:n * tall + 2 + fr, :] = tile[n, :, j * 128:(j + 1) * 128].astype(F32)
+
+    near = fl // LON_UP
+    picked_cols = [-1, 0, near - 1, near]
+    select_lane = lax.broadcasted_iota(jnp.int32, (cw, 128), 0)
+    select_pos = lax.broadcasted_iota(jnp.int32, (cw, 128), 1)
+    hits = jnp.zeros((cw, 128), jnp.bool_)
+    for s, col in enumerate(picked_cols):
+        hits = jnp.logical_or(hits, jnp.logical_and(select_pos == s, select_lane == col % cw))
+    chosen[...] = jnp.where(hits, 1.0, 0.0).astype(BF16)
+    key = lax.broadcasted_iota(jnp.int32, (128, 1), 0)
+    key_line = key // 4
+    key_pick = key - 4 * key_line
+    key_col = jnp.where(key_pick == 0, picked_cols[0], jnp.where(
+        key_pick == 1, picked_cols[1], jnp.where(key_pick == 2, picked_cols[2], picked_cols[3])))
+    edge_row = jnp.where(lane < HALF, lane, lane - HALF)
+    for p in range(3):
+        a, b, share, ok = lat_split(edge_row + p, top, bottom, count, r * fr, fr * tile_rows)
+        wa = jnp.where(ok, 1.0 - share, 0.0)
+        wb = jnp.where(ok, share, 0.0)
+        by_row = jnp.where(key_line == a, wa, 0.0) + jnp.where(key_line == b, wb, 0.0)
+        for q in range(3):
+            lower_col, share_m = lon_split(jnp.where(lane < HALF, q - 2, fl - 1 + q))
+            by_col = jnp.where(key_col == lower_col, 1.0 - share_m, jnp.where(key_col == lower_col + 1, share_m, 0.0))
+            sidew[3 * p + q] = (by_row * by_col).astype(BF16)
+
     own.wait()
 
     def arrived(slot, span_rows=whole):
@@ -239,56 +302,6 @@
         arrived(6)
         arrived(7, upper)
 
-    def real(i):
-        row = r * (lines_n - 2 * spare) - spare + i
-        return jnp.logical_and(row >= 0, row < (lines_n - 2 * spare) * tile_rows)
-
-    half_gains = [column(gain[k:k + 1, :])[:, :1] * 0.5 for k in range(blocks)]
-    biases = [column(regb[k:k + 1, :])[:, :1] for k in range(blocks)]
-
-    def spread(k, i, values):
-        values = activate(values, half_gains[k])
-        taps = jnp.concatenate(
-            [pltpu.roll(values, 1, 1).astype(BF16), values.astype(BF16), pltpu.roll(values, cw - 1, 1).astype(BF16)],
-            axis=0)
-        part[k % 2, i] = jnp.dot(regw[k], taps, preferred_element_type=F32)
-
-    def enter(i, _):
-        own_cols = got[i, :cin, :].astype(F32)
-        side = got[i, cin:, :].astype(F32)
-        outer = []
-        for g in range(cin // 16):
-            after = pltpu.roll(side, 128 - halo - g * span - 2 * halo * east, 1)
-            before = pltpu.roll(side, 128 - halo - g * span - 2 * halo * c, 1)
-            outer.append(jnp.where(lane < halo, after, jnp.where(lane >= 128 - halo, before, 0.0)))
-        values = jnp.concatenate([own_cols, jnp.concatenate(outer, axis=0)], axis=1)
-        values = jnp.where(real(i), values, 0.0)
-        held[i] = values
-        spread(0, i, values)
-        return 0
-
-    lax.fori_loop(1, lines_n - 1, enter, 0, unroll=2)
-
-    def update(k, i):
-        values = held[i] + part[k % 2, i - 1, :cin, :] + part[k % 2, i, cin:2 * cin, :] + part[k % 2, i + 1, 2 * cin:, :]
-        values = (values + biases[k]).astype(BF16)
-        return jnp.where(real(i), values.astype(F32), 0.0)
-
-    for k in range(1, blocks):
-        def follow(i, _, k=k):
-            values = update(k - 1, i)
-            held[i] = values
-            spread(k, i, values)
-            return 0
-
-        lax.fori_loop(1 + k, lines_n - 1 - k, follow, 0, unroll=2)
-
-    def leave(i, _):
-        field[i - halo] = update(blocks - 1, i).astype(BF16)
-        return 0
-
-    lax.fori_loop(halo, lines_n - halo, leave, 0, unroll=2)
-
     edge(0)
     edge(1)
 
@@ -302,27 +315,20 @@
         for slot in (4, 5, 7, 9):
             edge(slot)
 
-    def along(middle, above, below):
-        above = jnp.where(top, 0.0, pltpu.roll(above.astype(F32), 128 - (fr - 2), 1))
-        below = jnp.where(bottom, 0.0, pltpu.roll(below.astype(F32), fr + 2, 1))
-        middle = pltpu.roll(middle.astype(F32), 2, 1)
-        return jnp.where(lane < 2, above, jnp.where(lane < fr + 2, middle, below))
-
-    ring[0] = along(got_cols[0], got_cols[2], got_cols[4])
-    ring[1] = along(got_cols[1], got_cols[3], got_cols[5])
-    ring[2] = along(cols[...], got_cols[6], got_cols[7])
-    got_rows[...] = far_rows[...]
+    for n in range(nout):
+        for j in range(wide):
+            at = slice(j * 128, (j + 1) * 128)
+            above = far_rows[0, :, at].astype(F32)[4 * n + 2:4 * n + 4]
+            below = far_rows[1, :, at].astype(F32)[4 * n:4 * n + 2]
+            grid[j, n * tall:n * tall + 2, :] = jnp.where(top, 0.0, above)
+            grid[j, n * tall + 2 + fr:(n + 1) * tall, :] = jnp.where(bottom, 0.0, below)
+
     each_band(lambda copy: copy.wait_send())
     each_edge(lambda copy: copy.wait_send())
 
 
-def lon_split(fine_col):
-    lower, part = split(2 * fine_col + 1 - LON_UP + 2 * LON_UP, LON_UP)
-    return lower - 1, part
-
-
-def first_program(coarse, noisy, gain, regb, regs, lifts, mids):
-    any_space = pl.BlockSpec(memory_space=pl.ANY)
+def first_program(coarse, noisy, gain, regb, regs, liftb, midg, midb, lifts, mids):
+    hbm = pl.BlockSpec(memory_space=pltpu.HBM)
     vmem = pl.BlockSpec(memory_space=pltpu.VMEM)
     dma = pltpu.SemaphoreType.DMA
     cin, band_rows, clon = coarse.shape
@@ -331,7 +337,6 @@
     blocks = regs.shape[0] // 9
     slab = 3 * cin + -(-3 * nout // 16) * 16
     lines_n = band_rows * (TILE_COLS + 4)
-    count = lines_n - 2 * (blocks + 1)
     ct_lon = clon // TILE_COLS
     cw = 2 * ct_lon
     assert ct_lon == 128 and cin % 16 == 0 and band_rows == 2
@@ -340,87 +345,126 @@
     return pl.pallas_call(
         first_kernel,
         out_shape=(
-            shape((count, cin, cw), BF16),
-            shape((3, 4 * nout, 128), F32),
-            shape((2, 4 * nout, fl), BF16),
+            shape((lines_n, cin + 16, 128), BF16),
+            shape((8, 4 * nout, 128), BF16),
+            shape((4 * nout, 128), BF16),
+            shape((fl // 128, nout * (fr + 4), 128), F32),
+            shape((blocks, 3 * cin, 3 * cin), BF16),
+            shape((2 * blocks, cin, 128), F32),
             shape((ch, 3 * slab), BF16),
+            shape((3, ch, 128), F32),
             shape((ch, 9 * ch), BF16),
             shape((cw, 3 * fl), BF16),
+            shape((9, 128, 128), BF16),
+            shape((cw, 128), BF16),
         ),
-        in_specs=[any_space] * 2 + [vmem] * 2 + [any_space] * 3,
-        out_specs=(vmem,) * 6,
+        in_specs=[hbm] * 10,
+        out_specs=(vmem,) * 12,
         scratch_shapes=[
             pltpu.VMEM((cin, band_rows, clon), BF16),
             pltpu.VMEM((TILE_COLS, band_rows, cin + 16, 128), BF16),
-            pltpu.VMEM((lines_n, cin + 16, 128), BF16),
             pltpu.VMEM((nout, fr, fl), BF16),
-            pltpu.VMEM((4 * nout, 128), BF16),
             pltpu.VMEM((4 * nout, fl), BF16),
-            pltpu.VMEM((8, 4 * nout, 128), BF16),
             pltpu.VMEM((2, 4 * nout, fl), BF16),
+            pltpu.VMEM(gain.shape, F32),
+            pltpu.VMEM(regb.shape, F32),
+            pltpu.VMEM((3, 1, ch), F32),
             pltpu.VMEM(regs.shape, BF16),
             pltpu.VMEM(lifts.shape, BF16),
             pltpu.VMEM(mids.shape, BF16),
-            pltpu.VMEM((blocks, 3 * cin, 3 * cin), BF16),
             pltpu.VMEM((3 * slab, ch), BF16),
-            pltpu.VMEM((lines_n, cin, cw), F32),
-            pltpu.VMEM((2, lines_n, 3 * cin, cw), F32),
-            dma((2 * TILE_COLS,)), dma((8,)), dma((10,)), dma((10,)), dma((6,)),
+            dma((2 * TILE_COLS,)), dma((8,)), dma((10,)), dma((10,)), dma((11,)),
         ],
         compiler_params=pltpu.CompilerParams(
-            collective_id=0, has_side_effects=True, vmem_limit_bytes=24_000_000),
-    )(coarse, noisy, gain, regb, regs, lifts, mids)
+            collective_id=0, has_side_effects=True, vmem_limit_bytes=20_000_000),
+    )(*[pltpu.with_memory_space_constraint(x, pltpu.HBM) for x in (
+        coarse, noisy, gain, regb, regs, liftb, midg, midb, lifts, mids)])
 
 
 def tile_kernel(
-    dims, field, tile, ring, got_rows, liftw, liftb, midg, midw, midb, lon, out,
-    grid, lines, upper, sides, bands, keep, raw, prod, edges, cols, rows_out, stage, sems,
+    dims, got, got_cols, own_cols, grid, regw, regc, liftw, cols, midw, lon, sidew, chosen, out,
+    held, part, field, lines, upper, sides, bands, keep, raw, prod, edges, rows_out, stage, sems,
 ):
-    cin, ch, fr, fl = dims
-    count, cw = field.shape[0], field.shape[2]
-    tile_row, tile_rows = lax.axis_index("lat") // TILE_COLS, lax.axis_size("lat") // TILE_COLS
-    nout = tile.shape[1]
+    cin, ch, nout, fr, fl = dims
+    lines_n, count, cw = got.shape[0], field.shape[0], field.shape[2]
+    blocks = regw.shape[0]
+    halo = blocks + 1
+    span = 2 * halo * TILE_COLS
+    me = lax.axis_index("lat")
+    tile_row, tile_rows = me // TILE_COLS, lax.axis_size("lat") // TILE_COLS
+    c = me % TILE_COLS
+    after_seam = (c + 1) % TILE_COLS
     top, bottom = tile_row == 0, tile_row == tile_rows - 1
     steps = bands.shape[0]
     wide = fl // 128
-
-    cols[0] = column(liftb[...])
-    cols[1] = column(midg[...]) * 0.5
-    cols[2] = column(midb[...])
+    lane = lax.broadcasted_iota(jnp.int32, (1, 128), 1)
+    lane_first, lane_last = lane == 0, lane == 127
+    spare = lines_n // 4
+
+    def known(i, values):
+        if i < spare:
+            return jnp.where(top, 0.0, values)
+        if i >= lines_n - spare:
+            return jnp.where(bottom, 0.0, values)
+        return values
+
+    def spread(k, i, values):
+        values = activate(values, regc[2 * k][:, :1])
+        taps = jnp.concatenate(
+            [pltpu.roll(values, 1, 1).astype(BF16), values.astype(BF16), pltpu.roll(values, cw - 1, 1).astype(BF16)],
+            axis=0)
+        part[k % 2, i] = jnp.dot(regw[k], taps, preferred_element_type=F32)
+
+    for i in range(1, lines_n - 1):
+        side = got[i, cin:, :].astype(F32)
+        outer = []
+        for g in range(cin // 16):
+            after = pltpu.roll(side, 128 - halo - g * span - 2 * halo * after_seam, 1)
+            before = pltpu.roll(side, 128 - halo - g * span - 2 * halo * c, 1)
+            outer.append(jnp.where(lane < halo, after, jnp.where(lane >= 128 - halo, before, 0.0)))
+        values = jnp.concatenate([got[i, :cin, :].astype(F32), jnp.concatenate(outer, axis=0)], axis=1)
+        values = known(i, values)
+        held[i] = values
+        spread(0, i, values)
+
+    def update(k, i):
+        values = held[i] + part[k % 2, i - 1, :cin, :] + part[k % 2, i, cin:2 * cin, :] + part[k % 2, i + 1, 2 * cin:, :]
+        values = (values + regc[2 * k + 1][:, :1]).astype(BF16)
+        return known(i, values.astype(F32))
+
+    for k in range(1, blocks):
+        for i in range(1 + k, lines_n - 1 - k):
+            values = update(k - 1, i)
+            held[i] = values
+            spread(k, i, values)
+
+    for i in range(halo, lines_n - halo):
+        field[i - halo] = update(blocks - 1, i).astype(BF16)
 
     for q in range(3):
         lines[:, q * cin:(q + 1) * cin, :] = jnp.dot(
             field[...].reshape(count * cin, cw), lon[:, q * fl:(q + 1) * fl],
             preferred_element_type=F32).reshape(count, cin, fl)
 
-    low_line = jnp.where(top, 1, 0)
-    high_line = jnp.where(bottom, count - 2, count - 1)
-    fine_total = fr * tile_rows
+    def blend(t):
+        return lat_split(t, top, bottom, count, tile_row * fr, fr * tile_rows)
 
     def inside(t):
         row = tile_row * fr + t - 2
-        return jnp.logical_and(row >= 0, row < fine_total)
-
-    def lat_split(t):
-        lower, part = split(2 * (t - 2) + 1 - LAT_UP + 2 * LAT_UP, LAT_UP)
-        return jnp.clip(lower, low_line, high_line), jnp.clip(lower + 1, low_line, high_line), part
-
+        return jnp.logical_and(row >= 0, row < fr * tile_rows)
+
+    tall = fr + 4
     slab = upper.shape[1]
-    lane = lax.broadcasted_iota(jnp.int32, (1, 128), 1)
-    lane_first, lane_last = lane == 0, lane == 127
-
-    tall = fr + 4
-    for n in range(nout):
-        for j in range(wide):
-            at = slice(j * 128, (j + 1) * 128)
-            base = n * tall
-            grid[j, base + 2:base + 2 + fr, :] = tile[0, n, :, at].astype(F32)
-            above = got_rows[0, :, at].astype(F32)[4 * n + 2:4 * n + 4]
-            below = got_rows[1, :, at].astype(F32)[4 * n:4 * n + 2]
-            grid[j, base:base + 2, :] = jnp.where(top, 0.0, above)
-            grid[j, base + 2 + fr:base + tall, :] = jnp.where(bottom, 0.0, below)
-
-    west, east, here = ring[0], ring[1], ring[2]
+
+    def along(middle, above, below):
+        above = jnp.where(top, 0.0, pltpu.roll(above.astype(F32), 128 - (fr - 2), 1))
+        below = jnp.where(bottom, 0.0, pltpu.roll(below.astype(F32), fr + 2, 1))
+        middle = pltpu.roll(middle.astype(F32), 2, 1)
+        return jnp.where(lane < 2, above, jnp.where(lane < fr + 2, middle, below))
+
+    west = along(got_cols[0], got_cols[2], got_cols[4])
+    east = along(got_cols[1], got_cols[3], got_cols[5])
+    here = along(own_cols[...], got_cols[6], got_cols[7])
     none = jnp.zeros((slab - 3 * (cin + nout), 128), F32)
     left_cols = jnp.concatenate([west[2 * nout:], here[:nout], none], axis=0)
     right_cols = jnp.concatenate([here[3 * nout:], east[:2 * nout], none], axis=0)
@@ -440,46 +484,23 @@
         return jnp.concatenate(pieces, axis=1).astype(BF16)
 
     def raise_row(t, slot):
-        a, b, part = lat_split(jnp.int32(t))
-        ok = inside(t)
-        wa = jnp.where(ok, 1.0 - part, 0.0)
-        wb = jnp.where(ok, part, 0.0)
+        a, b, share, ok = blend(jnp.int32(t))
+        wa = jnp.where(ok, 1.0 - share, 0.0)
+        wb = jnp.where(ok, share, 0.0)
         for o in range(0, 3 * cin, 16):
             upper[slot, o:o + 16, :] = (wa * lines[a, o:o + 16, :] + wb * lines[b, o:o + 16, :]).astype(BF16)
         upper[slot, 3 * cin:slab, :] = noise_rows(t)
 
     edge_row = jnp.where(lane < HALF, lane, lane - HALF)
-    near = fl // LON_UP
-    picked_cols = [-1, 0, near - 1, near]
-    select_lane = lax.broadcasted_iota(jnp.int32, (cw, 128), 0)
-    select_pos = lax.broadcasted_iota(jnp.int32, (cw, 128), 1)
-    hits = jnp.zeros((cw, 128), jnp.bool_)
-    for s, col in enumerate(picked_cols):
-        hits = jnp.logical_or(hits, jnp.logical_and(select_pos == s, select_lane == col % cw))
-    chosen = jnp.where(hits, 1.0, 0.0).astype(BF16)
-    packed = jnp.zeros((cin, 128), F32)
-    for i in range(count):
-        narrow = jnp.dot(field[i], chosen, preferred_element_type=F32)
-        packed = packed + (pltpu.roll(narrow, 4 * i, 1) if i else narrow)
+    narrow = jnp.dot(field[...].reshape(count * cin, cw), chosen[...], preferred_element_type=F32)
+    packed = narrow[:cin]
+    for i in range(1, count):
+        packed = packed + pltpu.roll(narrow[i * cin:(i + 1) * cin], 4 * i, 1)
     packed = packed.astype(BF16)
-    key = lax.broadcasted_iota(jnp.int32, (128, 1), 0)
-    key_line = key // 4
-    key_pick = key - 4 * key_line
-    key_col = jnp.where(key_pick == 0, picked_cols[0], jnp.where(
-        key_pick == 1, picked_cols[1], jnp.where(key_pick == 2, picked_cols[2], picked_cols[3])))
     for p in range(3):
-        t = edge_row + p
-        a, b, part = lat_split(t)
-        ok = inside(t)
-        wa = jnp.where(ok, 1.0 - part, 0.0)
-        wb = jnp.where(ok, part, 0.0)
-        by_row = jnp.where(key_line == a, wa, 0.0) + jnp.where(key_line == b, wb, 0.0)
         for q in range(3):
-            lower, part_m = lon_split(jnp.where(lane < HALF, q - 2, fl - 1 + q))
-            by_col = jnp.where(key_col == lower, 1.0 - part_m, jnp.where(key_col == lower + 1, part_m, 0.0))
             base = p * slab + q * cin
-            sides[base:base + cin, :] = jnp.dot(
-                packed, (by_row * by_col).astype(BF16), preferred_element_type=F32).astype(BF16)
+            sides[base:base + cin, :] = jnp.dot(packed, sidew[3 * p + q], preferred_element_type=F32).astype(BF16)
         sides[p * slab + 3 * cin:(p + 1) * slab, :] = jnp.where(
             lane < HALF, pltpu.roll(left_cols, (128 - p) % 128, 1), pltpu.roll(right_cols, HALF - p, 1)).astype(BF16)
     edge_lift = jnp.dot(liftw[...], sides[...], preferred_element_type=F32) + cols[0]
@@ -524,79 +545,107 @@
         prod[slot % 2] = jnp.dot(midw[...], window, preferred_element_type=F32)
 
     group = stage.shape[2]
-
-    def flush(part):
-        slot = part % 2
-
-        def copy(n):
-            return pltpu.make_async_copy(
-                stage.at[n % 2], out.at[0, :, pl.ds(pl.multiple_of(n * group, group), group), :], sems.at[n % 2])
-
-        @pl.when(part >= 2)
-        def _():
-            copy(part - 2).wait()
-
-        def shrink(o, _):
-            for j in range(wide):
-                block = rows_out[j, pl.ds(pl.multiple_of(o * 8 * group, 8 * group), 8 * group), :]
-                stage[slot, pl.ds(o * 8, 8), :, j * 128:(j + 1) * 128] = block.reshape(8, group, 128).astype(BF16)
-            return 0
-
-        lax.fori_loop(0, ch // 8, shrink, 0)
-        copy(part).start()
-
-    def emit(y, slot):
-        spot = y % group
+    blocks_out = ch // 8
+
+    def flushed(n):
+        return pltpu.make_async_copy(
+            stage.at[n % 2], out.at[0, :, pl.ds(pl.multiple_of(n * group, group), group), :], sems.at[n % 2])
+
+    def shrink(n, o):
+        for j in range(wide):
+            block = rows_out[n % 2, j, pl.ds(pl.multiple_of(o * 8 * group, 8 * group), 8 * group), :]
+            stage[n % 2, pl.ds(o * 8, 8), :, j * 128:(j + 1) * 128] = block.reshape(8, group, 128).astype(BF16)
+
+    def emit(n, spot, slot):
         for o in range(0, ch, 16):
             bias = cols[2, o:o + 16, :]
             for j in range(wide):
                 at = slice(j * 128, (j + 1) * 128)
                 total = keep[(slot + 1) % steps, o:o + 16, at].astype(F32) + prod[slot % 2, o:o + 16, at] + bias
-                rows_out[j, pl.ds(spot + o * group, 16, stride=group), :] = total
+                rows_out[n % 2, j, pl.ds(spot + o * group, 16, stride=group), :] = total
 
     for t in range(3):
         raise_row(t, t % steps)
-    for l in range(3):
+    for l in range(5):
         lift(l % steps)
         raise_row(l + 3, (l + 3) % steps)
-        finish(jnp.int32(l), l % steps)
+        if l:
+            finish(jnp.int32(l - 1), (l - 1) % steps)
+    mid(0)
+
+    halves = group // steps
+    share_out = blocks_out // group
+
+    def step(i, u, e, last):
+        n = i // halves
+        shrink_at = (i % halves) * (blocks_out // halves) + u * share_out
+        for o in range(share_out):
+            shrink(n + 1, shrink_at + o)
+        emit(n, (i % halves) * steps + u, u)
+        if last is None or last + 1 < fr:
+            mid((u + 1) % steps)
+        if last is None or last + 4 < fr + 2:
+            finish(e + 4, (u + 4) % steps)
+        if last is None or last + 5 < fr + 2:
+            lift((u + 5) % steps)
+        if last is None:
+            raise_row(e + 8, u)
+
+    trips = fr // steps
+
+    def begin(i):
+        @pl.when(jnp.logical_and(i % halves == 0, i >= 3 * halves))
+        def _():
+            flushed(i // halves - 3).wait()
+
+    def finish_trip(i):
+        @pl.when(jnp.logical_and(i % halves == halves - 1, i >= halves))
+        def _():
+            flushed(i // halves - 1).start()
 
     def trip(i, _):
-        for j in range(steps):
-            l = i * steps + j + 3
-            slot = (j + 3) % steps
-            lift(slot)
-            mid(j)
-            raise_row(jnp.minimum(l + 3, fr + 3), (j + 6) % steps)
-            finish(l, slot)
-            emit(l - 3, j)
-
-        @pl.when((i + 1) % (group // steps) == 0)
-        def _():
-            flush(i // (group // steps))
+        begin(i)
+        for u in range(steps):
+            step(i, u, i * steps + u, None)
+        finish_trip(i)
         return 0
 
-    lax.fori_loop(0, fr // steps, trip, 0)
-    parts = fr // group
-    for n in range(max(parts - 2, 0), parts):
-        pltpu.make_async_copy(stage.at[n % 2], out.at[0, :, pl.ds(n * group, group), :], sems.at[n % 2]).wait()
-
-
-def tile_program(field, noisy, ring, got_rows, liftw, liftb, midg, midw, midb, lon):
-    count, cin, cw = field.shape
-    ch = liftw.shape[0]
-    nout, fr, fl = noisy.shape[1:]
-    group = 16
+    lax.fori_loop(0, trips - 1, trip, 0)
+    i = jnp.int32(trips - 1)
+    begin(i)
+    for u in range(steps):
+        step(i, u, i * steps + u, fr - steps + u)
+    finish_trip(i)
+    groups = fr // group
+    if groups >= 3:
+        flushed(groups - 3).wait()
+    for o in range(blocks_out):
+        shrink(groups - 1, o)
+    flushed(groups - 1).start()
+    for n in range(max(groups - 2, 0), groups):
+        flushed(n).wait()
+
+
+def tile_program(dims, prepared):
+    cin, ch, nout, fr, fl = dims
+    got, lon, liftw = prepared[0], prepared[9], prepared[6]
+    lines_n = got.shape[0]
+    cw = lon.shape[0]
+    blocks = prepared[4].shape[0]
+    count = lines_n - 2 * (blocks + 1)
+    group = 8
     steps = 4
     vmem = pl.BlockSpec(memory_space=pltpu.VMEM)
     slab = liftw.shape[1] // 3
     return pl.pallas_call(
-        functools.partial(tile_kernel, (cin, ch, fr, fl)),
+        functools.partial(tile_kernel, dims),
         out_shape=jax.ShapeDtypeStruct((1, ch, fr, fl), BF16),
-        in_specs=[vmem] * 10,
+        in_specs=[vmem] * len(prepared),
         out_specs=pl.BlockSpec(memory_space=pl.ANY),
         scratch_shapes=[
-            pltpu.VMEM((fl // 128, nout * (fr + 4), 128), F32),
+            pltpu.VMEM((lines_n, cin, cw), F32),
+            pltpu.VMEM((2, lines_n, 3 * cin, cw), F32),
+            pltpu.VMEM((count, cin, cw), BF16),
             pltpu.VMEM((count, 3 * cin, fl), F32),
             pltpu.VMEM((steps, slab, fl), BF16),
             pltpu.VMEM((3 * slab, 128), BF16),
@@ -605,24 +654,23 @@
             pltpu.VMEM((2, ch, fl), F32),
             pltpu.VMEM((2, ch, fl), F32),
             pltpu.VMEM((ch, 128), F32),
-            pltpu.VMEM((3, ch, 128), F32),
-            pltpu.VMEM((fl // 128, ch * group, 128), F32),
+            pltpu.VMEM((2, fl // 128, ch * group, 128), F32),
             pltpu.VMEM((2, ch, group, fl), BF16),
             pltpu.SemaphoreType.DMA((2,)),
         ],
-        compiler_params=pltpu.CompilerParams(vmem_limit_bytes=40_000_000),
-    )(field, noisy, ring, got_rows, liftw, liftb, midg, midw, midb, lon)
+        compiler_params=pltpu.CompilerParams(vmem_limit_bytes=44_000_000),
+    )(*prepared)
 
 
 def per_device(
     coarse, reg_gain, reg_weight, reg_bias, noisy, lift_weight, lift_bias, mid_gain, mid_weight, mid_bias,
 ):
     lifts = lift_weight.transpose(0, 1, 3, 2)
-    field, ring, got_rows, liftw, midw, lon = first_program(
+    prepared = first_program(
         coarse, noisy, reg_gain, reg_bias, reg_weight.reshape((-1,) + reg_weight.shape[3:]),
+        lift_bias[None], mid_gain[None], mid_bias[None],
         lifts.reshape((9,) + lifts.shape[2:]), mid_weight.reshape((9,) + mid_weight.shape[2:]))
-    return tile_program(
-        field, noisy, ring, got_rows, liftw, lift_bias[None], mid_gain[None], midw, mid_bias[None], lon)
+    return tile_program((coarse.shape[0], mid_weight.shape[2]) + noisy.shape[1:], prepared)
 
 
 def solution(mesh):

time: 56.7 us -> 40.8 us (0.72)
  local copies, waits for them, and re-layouts: 9.26 us -> 0 us
  Pallas kernels: 46.7 us -> 40.6 us
    unnamed x22 -> x0, local copies, waits for them, and re-layouts: 9.26 us -> none
    pallas_call x2, Pallas kernels: 46.7 us -> 40.6 us  [the longest x1 29.9 us: tile_program(): pl.pallas_call(functools.partial(tile_kernel, dims), out_shape=jax.ShapeD...]
where the time goes in v1:
time: 40.8 us; the launch traced here: 40.6 us
  Pallas kernels  40.6 us (100%)
    pallas_call x1, Pallas kernels, tile_program(): pl.pallas_call(functools.partial(tile_kernel, dims), out_shape=jax.ShapeD...  29.9 us
    pallas_call x1, Pallas kernels, first_program(): pl.pallas_call(first_kernel, out_shape=(shape((lines_n, cin + 16, 128), B...  10.7 us

profile of v1, /device:TPU:0, one launch (start us, length us, event | category | flops | bytes accessed | tf_op | source)
XLA Modules:
  0.0 40.6 jit_solution(15687074305900846500)
XLA Ops:
  0.0 10.7 %shard_map.100 = (bf16[16,96,128]{2,1,0:T(8,128)(2,1)S(1)}, bf16[8,16,128]{2,1,0:T(8,128)(2,1)S(1)}, bf16[16,128]{1,0:T(8,128)(2,1)S(1)}, f32[4,144,128]{2,1,0:T...) custom-call(bf16[80,2,512]{2,1,0:T(2,128)(2,1)} %coarse.1, ...), custom_call_target="tpu_custom_call" | custom-call | tf_op jit(solution)/shard_map/pallas_call | solution.py:345
  10.7 29.9 %shard_map.101 = bf16[1,192,32,512]{3,2,1,0:T(8,128)(2,1)} custom-call(bf16[16,96,128]{2,1,0:T(8,128)(2,1)S(1)} %get-tuple-element.17.got, bf16[8,16,128]{2,1,0:T(8,128)(2,1)S(1)} %get-tuple-element.18.got_cols, bf16[16,128]{1,0:T(8,128)(2,1)S(1)} %get-tuple-element.19.own_cols, f32[4,144,128]{2,1,0:T(8,128)S(1)} %get-tuple-element.20.grid, ...), custom_call_target="tpu_custom_call" | custom-call | tf_op jit(solution)/shard_map/pallas_call | solution.py:640

commit v2 on v1

--- a/solution.py
+++ b/solution.py
@@ -32,6 +32,12 @@
     n = row.shape[1]
     here = lax.broadcasted_iota(jnp.int32, (n, n), 0) == lax.broadcasted_iota(jnp.int32, (n, n), 1)
     return jnp.broadcast_to(jnp.sum(jnp.where(here, row, 0.0), axis=1, keepdims=True), (n, 128))
+
+
+def thirds(values):
+    high = values.astype(BF16).astype(F32)
+    middle = (values - high).astype(BF16).astype(F32)
+    return [high, middle, values - high - middle]
 
 
 def nt_dot(a, b):
@@ -217,7 +223,8 @@
     loads[3].wait()
     for tap in range(9):
         midw[:, tap * ch:(tap + 1) * ch] = midv[tap]
-    loads[4].wait()
+    for load in loads[4:]:
+        load.wait()
     slab = liftt.shape[0] // 3
     for p in range(3):
         noise = []
@@ -225,7 +232,11 @@
             base = p * slab + q * cin
             liftt[base:base + cin, :] = liftv[3 * p + q, :cin, :]
             noise.append(liftv[3 * p + q, cin:, :].astype(F32))
-        noise.append(jnp.zeros((slab - 3 * (cin + nout), ch), F32))
+        spare_rows = slab - 3 * (cin + nout)
+        if p == 1:
+            noise += thirds(vecs[0]) + [jnp.zeros((spare_rows - 3, ch), F32)]
+        else:
+            noise.append(jnp.zeros((spare_rows, ch), F32))
         liftt[p * slab + 3 * cin:(p + 1) * slab, :] = jnp.concatenate(noise, axis=0).astype(BF16)
     eye = jnp.where(lax.broadcasted_iota(jnp.int32, (ch, ch), 0) == lax.broadcasted_iota(jnp.int32, (ch, ch), 1), 1.0, 0.0)
     liftw[...] = nt_dot(eye.astype(BF16), liftt[...]).astype(BF16)
@@ -239,14 +250,14 @@
     lon[...] = jnp.where(coarse_lane == low_lane, 1.0 - weight,
                          jnp.where(coarse_lane == high_lane, weight, 0.0)).astype(BF16)
 
-    for load in loads[5:]:
-        load.wait()
     for k in range(blocks):
         regc[2 * k] = column(gainv[k:k + 1, :]) * 0.5
         regc[2 * k + 1] = column(regbv[k:k + 1, :])
-    liftc[0] = column(vecs[0])
-    liftc[1] = column(vecs[1]) * 0.5
-    liftc[2] = column(vecs[2])
+    liftc[...] = column(vecs[1]) * 0.5
+    bias_cols = jnp.zeros((ch, 128), F32)
+    for n, third in enumerate(thirds(column(vecs[2]))):
+        bias_cols = jnp.where(lane == n, third, bias_cols)
+    midw[:, 9 * ch:] = bias_cols[:, :16].astype(BF16)
 
     tall = fr + 4
     wide = fl // 128
@@ -335,7 +346,7 @@
     nout, fr, fl = noisy.shape[1:]
     ch = mids.shape[1]
     blocks = regs.shape[0] // 9
-    slab = 3 * cin + -(-3 * nout // 16) * 16
+    slab = 3 * cin + -(-(3 * nout + 3) // 16) * 16
     lines_n = band_rows * (TILE_COLS + 4)
     ct_lon = clon // TILE_COLS
     cw = 2 * ct_lon
@@ -352,8 +363,8 @@
             shape((blocks, 3 * cin, 3 * cin), BF16),
             shape((2 * blocks, cin, 128), F32),
             shape((ch, 3 * slab), BF16),
-            shape((3, ch, 128), F32),
-            shape((ch, 9 * ch), BF16),
+            shape((ch, 128), F32),
+            shape((ch, 9 * ch + 16), BF16),
             shape((cw, 3 * fl), BF16),
             shape((9, 128, 128), BF16),
             shape((cw, 128), BF16),
@@ -382,8 +393,8 @@
 
 
 def tile_kernel(
-    dims, got, got_cols, own_cols, grid, regw, regc, liftw, cols, midw, lon, sidew, chosen, out,
-    held, part, field, lines, upper, sides, bands, keep, raw, prod, edges, rows_out, stage, sems,
+    dims, got, got_cols, own_cols, grid, regw, regc, liftw, gains, midw, lon, sidew, chosen, out,
+    held, part, field, lines, upper, sides, bands, unit, raw, prod, edges, rows_out, stage, sems,
 ):
     cin, ch, nout, fr, fl = dims
     lines_n, count, cw = got.shape[0], field.shape[0], field.shape[2]
@@ -415,7 +426,7 @@
             axis=0)
         part[k % 2, i] = jnp.dot(regw[k], taps, preferred_element_type=F32)
 
-    for i in range(1, lines_n - 1):
+    def enter(i):
         side = got[i, cin:, :].astype(F32)
         outer = []
         for g in range(cin // 16):
@@ -432,19 +443,16 @@
         values = (values + regc[2 * k + 1][:, :1]).astype(BF16)
         return known(i, values.astype(F32))
 
-    for k in range(1, blocks):
-        for i in range(1 + k, lines_n - 1 - k):
-            values = update(k - 1, i)
-            held[i] = values
-            spread(k, i, values)
-
-    for i in range(halo, lines_n - halo):
-        field[i - halo] = update(blocks - 1, i).astype(BF16)
-
-    for q in range(3):
-        lines[:, q * cin:(q + 1) * cin, :] = jnp.dot(
-            field[...].reshape(count * cin, cw), lon[:, q * fl:(q + 1) * fl],
-            preferred_element_type=F32).reshape(count, cin, fl)
+    def follow(k, i):
+        values = update(k - 1, i)
+        held[i] = values
+        spread(k, i, values)
+
+    def widen(first, last):
+        coarse = field[first:last].reshape((last - first) * cin, cw)
+        for q in range(3):
+            lines[first:last, q * cin:(q + 1) * cin, :] = jnp.dot(
+                coarse, lon[:, q * fl:(q + 1) * fl], preferred_element_type=F32).reshape(last - first, cin, fl)
 
     def blend(t):
         return lat_split(t, top, bottom, count, tile_row * fr, fr * tile_rows)
@@ -465,7 +473,7 @@
     west = along(got_cols[0], got_cols[2], got_cols[4])
     east = along(got_cols[1], got_cols[3], got_cols[5])
     here = along(own_cols[...], got_cols[6], got_cols[7])
-    none = jnp.zeros((slab - 3 * (cin + nout), 128), F32)
+    none = jnp.ones((slab - 3 * (cin + nout), 128), F32)
     left_cols = jnp.concatenate([west[2 * nout:], here[:nout], none], axis=0)
     right_cols = jnp.concatenate([here[3 * nout:], east[:2 * nout], none], axis=0)
     west_col, east_col = west[3 * nout:], east[:nout]
@@ -492,56 +500,52 @@
         upper[slot, 3 * cin:slab, :] = noise_rows(t)
 
     edge_row = jnp.where(lane < HALF, lane, lane - HALF)
-    narrow = jnp.dot(field[...].reshape(count * cin, cw), chosen[...], preferred_element_type=F32)
-    packed = narrow[:cin]
-    for i in range(1, count):
-        packed = packed + pltpu.roll(narrow[i * cin:(i + 1) * cin], 4 * i, 1)
-    packed = packed.astype(BF16)
-    for p in range(3):
-        for q in range(3):
-            base = p * slab + q * cin
-            sides[base:base + cin, :] = jnp.dot(packed, sidew[3 * p + q], preferred_element_type=F32).astype(BF16)
-        sides[p * slab + 3 * cin:(p + 1) * slab, :] = jnp.where(
-            lane < HALF, pltpu.roll(left_cols, (128 - p) % 128, 1), pltpu.roll(right_cols, HALF - p, 1)).astype(BF16)
-    edge_lift = jnp.dot(liftw[...], sides[...], preferred_element_type=F32) + cols[0]
-    edge_lift = edge_lift.astype(BF16).astype(F32)
-    edges[...] = jnp.where(inside(edge_row + 1), activate(edge_lift, cols[1]), 0.0)
-
-    def lift(slot):
+
+    def build_edges():
+        narrow = jnp.dot(field[...].reshape(count * cin, cw), chosen[...], preferred_element_type=F32)
+        packed = narrow[:cin]
+        for i in range(1, count):
+            packed = packed + pltpu.roll(narrow[i * cin:(i + 1) * cin], 4 * i, 1)
+        packed = packed.astype(BF16)
+        for p in range(3):
+            for q in range(3):
+                base = p * slab + q * cin
+                sides[base:base + cin, :] = jnp.dot(packed, sidew[3 * p + q], preferred_element_type=F32).astype(BF16)
+            sides[p * slab + 3 * cin:(p + 1) * slab, :] = jnp.where(
+                lane < HALF, pltpu.roll(left_cols, (128 - p) % 128, 1), pltpu.roll(right_cols, HALF - p, 1)).astype(BF16)
+        edge_lift = jnp.dot(liftw[...], sides[...], preferred_element_type=F32)
+        edges[...] = jnp.where(inside(edge_row + 1), activate(edge_lift, gains[...]), 0.0).astype(BF16)
+
+    def lift(slot, target):
         window = jnp.concatenate([upper[(slot + n) % steps] for n in range(3)], axis=0)
-        raw[slot % 2] = jnp.dot(liftw[...], window, preferred_element_type=F32)
+        raw[target % steps] = jnp.dot(liftw[...], window, preferred_element_type=F32)
 
     def finish(l, slot):
         squares = jnp.zeros((8, fl), F32)
         for o in range(0, ch, 16):
-            bias = jnp.concatenate([cols[0, o:o + 16, :]] * wide, axis=1)
-            rounded = (raw[slot % 2, o:o + 16, :] + bias).astype(BF16)
-            keep[slot, o:o + 16, :] = rounded
-            values = rounded.astype(F32)
+            values = raw[slot, o:o + 16, :]
             values = values * values
             squares = squares + (values[:8] + values[8:])
         inverse = lax.rsqrt(jnp.sum(squares, axis=0, keepdims=True) * (1.0 / ch) + EPSILON)
         inverse = jnp.where(inside(l + 1), inverse, 0.0)
         for o in range(0, ch, 16):
-            half_gain = jnp.concatenate([cols[1, o:o + 16, :]] * wide, axis=1)
-            half = keep[slot, o:o + 16, :].astype(F32) * inverse * half_gain
-            values = half + half * jnp.tanh(half)
+            half_gain = jnp.concatenate([gains[o:o + 16, :]] * wide, axis=1)
+            half = raw[slot, o:o + 16, :] * inverse * half_gain
+            values = (half + half * jnp.tanh(half)).astype(BF16)
             edge = edges[o:o + 16, :]
             parts = [values[:, j * 128:(j + 1) * 128] for j in range(wide)]
-            east = [pltpu.roll(v, 1, 1) for v in parts]
-            west = [pltpu.roll(v, 127, 1) for v in parts]
+            onward = [pltpu.roll(v, 1, 1) for v in parts]
+            back = [pltpu.roll(v, 127, 1) for v in parts]
             edge_l = pltpu.roll(edge, 128 - l, 1)
             edge_r = pltpu.roll(edge, 128 + HALF - 1 - l, 1)
-            bands[slot, ch + o:ch + o + 16, :] = values.astype(BF16)
+            bands[slot, ch + o:ch + o + 16, :] = values
             bands[slot, o:o + 16, :] = jnp.concatenate(
-                [jnp.where(lane_first, east[j - 1] if j else edge_l, east[j]) for j in range(wide)],
-                axis=1).astype(BF16)
+                [jnp.where(lane_first, onward[j - 1] if j else edge_l, onward[j]) for j in range(wide)], axis=1)
             bands[slot, 2 * ch + o:2 * ch + o + 16, :] = jnp.concatenate(
-                [jnp.where(lane_last, west[j + 1] if j < wide - 1 else edge_r, west[j]) for j in range(wide)],
-                axis=1).astype(BF16)
+                [jnp.where(lane_last, back[j + 1] if j < wide - 1 else edge_r, back[j]) for j in range(wide)], axis=1)
 
     def mid(slot):
-        window = jnp.concatenate([bands[(slot + n) % steps] for n in range(3)], axis=0)
+        window = jnp.concatenate([bands[(slot + n) % steps] for n in range(3)] + [unit[...]], axis=0)
         prod[slot % 2] = jnp.dot(midw[...], window, preferred_element_type=F32)
 
     group = stage.shape[2]
@@ -558,20 +562,52 @@
 
     def emit(n, spot, slot):
         for o in range(0, ch, 16):
-            bias = cols[2, o:o + 16, :]
             for j in range(wide):
                 at = slice(j * 128, (j + 1) * 128)
-                total = keep[(slot + 1) % steps, o:o + 16, at].astype(F32) + prod[slot % 2, o:o + 16, at] + bias
+                total = raw[(slot + 1) % steps, o:o + 16, at] + prod[slot % 2, o:o + 16, at]
                 rows_out[n % 2, j, pl.ds(spot + o * group, 16, stride=group), :] = total
 
-    for t in range(3):
+    unit[...] = jnp.ones(unit.shape, BF16)
+
+    def raised(t):
         raise_row(t, t % steps)
-    for l in range(5):
-        lift(l % steps)
-        raise_row(l + 3, (l + 3) % steps)
-        if l:
-            finish(jnp.int32(l - 1), (l - 1) % steps)
+
+    def lifted(l):
+        lift(l % steps, l)
+
+    def finished(l):
+        finish(jnp.int32(l), l % steps)
+
+    early = [[(raised, 0), (raised, 1), (raised, 2)], [(lifted, 0), (raised, 3)], [(lifted, 1), (raised, 4)],
+             [(lifted, 2), (raised, 5)], [(lifted, 3), (raised, 6)]]
+    widened = 0
+    for i in range(1, lines_n - 1):
+        enter(i)
+        for k in range(1, blocks):
+            if 1 + k <= i - k < lines_n - 1 - k:
+                follow(k, i - k)
+        row = i - blocks
+        if halo <= row < lines_n - halo:
+            field[row - halo] = update(blocks - 1, row).astype(BF16)
+            if (row - halo) % 2:
+                widen(widened, row - halo + 1)
+                widened = row - halo + 1
+            if widened >= 2 and early and (widened >= 4 or len(early) > 2):
+                for action, n in early.pop(0):
+                    action(n)
+    if widened < count:
+        widen(widened, count)
+    for actions in early:
+        for action, n in actions:
+            action(n)
+    build_edges()
+    finished(0)
+    lifted(4)
+    raised(7)
+    finished(1)
+    finished(2)
     mid(0)
+    finished(3)
 
     halves = group // steps
     share_out = blocks_out // group
@@ -587,7 +623,7 @@
         if last is None or last + 4 < fr + 2:
             finish(e + 4, (u + 4) % steps)
         if last is None or last + 5 < fr + 2:
-            lift((u + 5) % steps)
+            lift((u + 5) % steps, u + 5)
         if last is None:
             raise_row(e + 8, u)
 
@@ -650,10 +686,10 @@
             pltpu.VMEM((steps, slab, fl), BF16),
             pltpu.VMEM((3 * slab, 128), BF16),
             pltpu.VMEM((steps, 3 * ch, fl), BF16),
-            pltpu.VMEM((steps, ch, fl), BF16),
+            pltpu.VMEM((16, fl), BF16),
+            pltpu.VMEM((steps, ch, fl), F32),
             pltpu.VMEM((2, ch, fl), F32),
-            pltpu.VMEM((2, ch, fl), F32),
-            pltpu.VMEM((ch, 128), F32),
+            pltpu.VMEM((ch, 128), BF16),
             pltpu.VMEM((2, fl // 128, ch * group, 128), F32),
             pltpu.VMEM((2, ch, group, fl), BF16),
             pltpu.SemaphoreType.DMA((2,)),

time: 40.8 us -> 39.9 us (0.978)
  Pallas kernels: 40.6 us -> 39.7 us
    pallas_call x1, Pallas kernels: 29.9 us -> 29 us  [tile_program(): pl.pallas_call(functools.partial(tile_kernel, dims), out_shape=jax.ShapeD...]
where the time goes in v2:
time: 39.9 us; the launch traced here: 39.7 us
  Pallas kernels  39.7 us (99%)
    pallas_call x1, Pallas kernels, tile_program(): pl.pallas_call(functools.partial(tile_kernel, dims), out_shape=jax.ShapeD...  29 us
    pallas_call x1, Pallas kernels, first_program(): pl.pallas_call(first_kernel, out_shape=(shape((lines_n, cin + 16, 128), B...  10.7 us

profile of v2, /device:TPU:0, one launch (start us, length us, event | category | flops | bytes accessed | tf_op | source)
XLA Modules:
  0.0 39.7 jit_solution(8920706519040008421)
XLA Ops:
  0.0 10.7 %shard_map.100 = (bf16[16,96,128]{2,1,0:T(8,128)(2,1)S(1)}, bf16[8,16,128]{2,1,0:T(8,128)(2,1)S(1)}, bf16[16,128]{1,0:T(8,128)(2,1)S(1)}, f32[4,144,128]{2,1,0:T...) custom-call(bf16[80,2,512]{2,1,0:T(2,128)(2,1)} %coarse.1, ...), custom_call_target="tpu_custom_call" | custom-call | tf_op jit(solution)/shard_map/pallas_call | solution.py:356
  10.7 29.0 %shard_map.101 = bf16[1,192,32,512]{3,2,1,0:T(8,128)(2,1)} custom-call(bf16[16,96,128]{2,1,0:T(8,128)(2,1)S(1)} %get-tuple-element.17.got, bf16[8,16,128]{2,1,0:T(8,128)(2,1)S(1)} %get-tuple-element.18.got_cols, bf16[16,128]{1,0:T(8,128)(2,1)S(1)} %get-tuple-element.19.own_cols, f32[4,144,128]{2,1,0:T(8,128)S(1)} %get-tuple-element.20.grid, ...), custom_call_target="tpu_custom_call" | custom-call | tf_op jit(solution)/shard_map/pallas_call | solution.py:676

commit v3 on v2

--- a/solution.py
+++ b/solution.py
@@ -501,20 +501,30 @@
 
     edge_row = jnp.where(lane < HALF, lane, lane - HALF)
 
-    def build_edges():
-        narrow = jnp.dot(field[...].reshape(count * cin, cw), chosen[...], preferred_element_type=F32)
-        packed = narrow[:cin]
+    found = {}
+
+    def edge_pick():
+        found["narrow"] = jnp.dot(field[...].reshape(count * cin, cw), chosen[...], preferred_element_type=F32)
+
+    def edge_pack():
+        packed = found["narrow"][:cin]
         for i in range(1, count):
-            packed = packed + pltpu.roll(narrow[i * cin:(i + 1) * cin], 4 * i, 1)
-        packed = packed.astype(BF16)
-        for p in range(3):
-            for q in range(3):
-                base = p * slab + q * cin
-                sides[base:base + cin, :] = jnp.dot(packed, sidew[3 * p + q], preferred_element_type=F32).astype(BF16)
-            sides[p * slab + 3 * cin:(p + 1) * slab, :] = jnp.where(
-                lane < HALF, pltpu.roll(left_cols, (128 - p) % 128, 1), pltpu.roll(right_cols, HALF - p, 1)).astype(BF16)
-        edge_lift = jnp.dot(liftw[...], sides[...], preferred_element_type=F32)
-        edges[...] = jnp.where(inside(edge_row + 1), activate(edge_lift, gains[...]), 0.0).astype(BF16)
+            packed = packed + pltpu.roll(found["narrow"][i * cin:(i + 1) * cin], 4 * i, 1)
+        found["packed"] = packed.astype(BF16)
+
+    def edge_blend(p):
+        for q in range(3):
+            base = p * slab + q * cin
+            sides[base:base + cin, :] = jnp.dot(
+                found["packed"], sidew[3 * p + q], preferred_element_type=F32).astype(BF16)
+        sides[p * slab + 3 * cin:(p + 1) * slab, :] = jnp.where(
+            lane < HALF, pltpu.roll(left_cols, (128 - p) % 128, 1), pltpu.roll(right_cols, HALF - p, 1)).astype(BF16)
+
+    def edge_lift():
+        found["lift"] = jnp.dot(liftw[...], sides[...], preferred_element_type=F32)
+
+    def edge_finish():
+        edges[...] = jnp.where(inside(edge_row + 1), activate(found["lift"], gains[...]), 0.0).astype(BF16)
 
     def lift(slot, target):
         window = jnp.concatenate([upper[(slot + n) % steps] for n in range(3)], axis=0)
@@ -578,36 +588,32 @@
     def finished(l):
         finish(jnp.int32(l), l % steps)
 
-    early = [[(raised, 0), (raised, 1), (raised, 2)], [(lifted, 0), (raised, 3)], [(lifted, 1), (raised, 4)],
-             [(lifted, 2), (raised, 5)], [(lifted, 3), (raised, 6)]]
-    widened = 0
-    for i in range(1, lines_n - 1):
-        enter(i)
+    def settle(row):
+        field[row - halo] = update(blocks - 1, row).astype(BF16)
+
+    plan = []
+    lag = 3
+    for i in range(1, lines_n - 1 + lag * blocks):
+        if i < lines_n - 1:
+            plan.append((enter, i))
         for k in range(1, blocks):
-            if 1 + k <= i - k < lines_n - 1 - k:
-                follow(k, i - k)
-        row = i - blocks
+            row = i - lag * k
+            if 1 + k <= row < lines_n - 1 - k:
+                plan.append((functools.partial(follow, k), row))
+        row = i - lag * blocks
         if halo <= row < lines_n - halo:
-            field[row - halo] = update(blocks - 1, row).astype(BF16)
-            if (row - halo) % 2:
-                widen(widened, row - halo + 1)
-                widened = row - halo + 1
-            if widened >= 2 and early and (widened >= 4 or len(early) > 2):
-                for action, n in early.pop(0):
-                    action(n)
-    if widened < count:
-        widen(widened, count)
-    for actions in early:
-        for action, n in actions:
-            action(n)
-    build_edges()
-    finished(0)
-    lifted(4)
-    raised(7)
-    finished(1)
-    finished(2)
-    mid(0)
-    finished(3)
+            plan.append((settle, row))
+            line = row - halo
+            if line % 2:
+                plan.append((lambda n: widen(n - 1, n + 1), line))
+            elif line == count - 1:
+                plan.append((lambda n: widen(n, n + 1), line))
+    plan += [(lambda _: edge_pick(), 0), (raised, 0), (raised, 1), (lambda _: edge_pack(), 0), (raised, 2),
+             (lifted, 0), (raised, 3), (edge_blend, 0), (edge_blend, 1), (edge_blend, 2), (raised, 4), (lifted, 1), (raised, 5),
+             (lambda _: edge_lift(), 0), (lifted, 2), (raised, 6), (lambda _: edge_finish(), 0), (lifted, 3), (finished, 0),
+             (raised, 7), (finished, 1), (lifted, 4), (finished, 2), (mid, 0), (finished, 3)]
+    for action, n in plan:
+        action(n)
 
     halves = group // steps
     share_out = blocks_out // group

time: 39.9 us -> 38.2 us (0.957)
  Pallas kernels: 39.7 us -> 38.1 us
    pallas_call x1, Pallas kernels: 29 us -> 27.4 us  [tile_program(): pl.pallas_call(functools.partial(tile_kernel, dims), out_shape=jax.ShapeD...]
where the time goes in v3:
time: 38.2 us; the launch traced here: 38.1 us
  Pallas kernels  38.1 us (100%)
    pallas_call x1, Pallas kernels, tile_program(): pl.pallas_call(functools.partial(tile_kernel, dims), out_shape=jax.ShapeD...  27.4 us
    pallas_call x1, Pallas kernels, first_program(): pl.pallas_call(first_kernel, out_shape=(shape((lines_n, cin + 16, 128), B...  10.7 us

profile of v3, /device:TPU:0, one launch (start us, length us, event | category | flops | bytes accessed | tf_op | source)
XLA Modules:
  0.0 38.1 jit_solution(12371577489001989196)
XLA Ops:
  0.0 10.7 %shard_map.100 = (bf16[16,96,128]{2,1,0:T(8,128)(2,1)S(1)}, bf16[8,16,128]{2,1,0:T(8,128)(2,1)S(1)}, bf16[16,128]{1,0:T(8,128)(2,1)S(1)}, f32[4,144,128]{2,1,0:T...) custom-call(bf16[80,2,512]{2,1,0:T(2,128)(2,1)} %coarse.1, ...), custom_call_target="tpu_custom_call" | custom-call | tf_op jit(solution)/shard_map/pallas_call | solution.py:356
  10.7 27.4 %shard_map.101 = bf16[1,192,32,512]{3,2,1,0:T(8,128)(2,1)} custom-call(bf16[16,96,128]{2,1,0:T(8,128)(2,1)S(1)} %get-tuple-element.17.got, bf16[8,16,128]{2,1,0:T(8,128)(2,1)S(1)} %get-tuple-element.18.got_cols, bf16[16,128]{1,0:T(8,128)(2,1)S(1)} %get-tuple-element.19.own_cols, f32[4,144,128]{2,1,0:T(8,128)S(1)} %get-tuple-element.20.grid, ...), custom_call_target="tpu_custom_call" | custom-call | tf_op jit(solution)/shard_map/pallas_call | solution.py:682

commit v4 on v3

--- a/solution.py
+++ b/solution.py
@@ -58,9 +58,36 @@
     return jnp.clip(lower, low_line, high_line), jnp.clip(lower + 1, low_line, high_line), part, ok
 
 
+def gather_row(got, i, c, halo):
+    cin = got.shape[1] - 16
+    lane = lax.broadcasted_iota(jnp.int32, (1, 128), 1)
+    span = 2 * halo * TILE_COLS
+    side = got[i, cin:, :].astype(F32)
+    outer = []
+    for g in range(cin // 16):
+        after = pltpu.roll(side, 128 - halo - g * span - 2 * halo * ((c + 1) % TILE_COLS), 1)
+        before = pltpu.roll(side, 128 - halo - g * span - 2 * halo * c, 1)
+        outer.append(jnp.where(lane < halo, after, jnp.where(lane >= 128 - halo, before, 0.0)))
+    return jnp.concatenate([got[i, :cin, :].astype(F32), jnp.concatenate(outer, axis=0)], axis=1)
+
+
+def convolve(values, half_gain, weight):
+    cw = values.shape[1]
+    values = activate(values, half_gain[:, :1])
+    taps = jnp.concatenate(
+        [pltpu.roll(values, 1, 1).astype(BF16), values.astype(BF16), pltpu.roll(values, cw - 1, 1).astype(BF16)],
+        axis=0)
+    return jnp.dot(weight, taps, preferred_element_type=F32)
+
+
+def add_rows(values, above, here, below, bias):
+    cin = values.shape[0]
+    return (values + above[:cin] + here[cin:2 * cin] + below[2 * cin:] + bias[:, :1]).astype(BF16)
+
+
 def first_kernel(
     coarse, noisy, gain, regb, regs, liftb, midg, midb, lifts, mids,
-    got, got_cols, cols, grid, regw, regc, liftw, liftc, midw, lon, sidew, chosen,
+    got, got_cols, cols, grid, regw, regc, liftw, liftc, midw, lon, sidew, chosen, held, part, field,
     band, pieces, tile, rows, far_rows, gainv, regbv, vecs, regv, liftv, midv, liftt,
     send, recv, nsend, nrecv, local,
 ):
@@ -165,8 +192,14 @@
     def landing(slot, span_rows):
         return got.at[pl.ds(2 * slot + span_rows[0], span_rows[1])]
 
+    def far_first(k):
+        return ((c // 2) * 2 + 2 + k) % TILE_COLS
+
+    def beside():
+        return c + 1 - 2 * (c % 2)
+
     def band_copy(k, row, slot, ssem, span_rows=whole):
-        col = (c + k) % TILE_COLS
+        col = far_first(k)
         return remote(pieces.at[col, pl.ds(*span_rows)], landing(slot, span_rows), send.at[ssem], recv.at[slot],
                       row * TILE_COLS + col)
 
@@ -188,8 +221,10 @@
                 for k in range(TILE_COLS):
                     action(band_copy(k, row, slot, TILE_COLS + k, span_rows))
 
-        for k in range(1, TILE_COLS):
+        for k in range(TILE_COLS - 2):
             action(band_copy(k, r, 2 + c, k))
+        action(remote(pieces.at[beside(), pl.ds(0, 2)], landing(2 + c, whole), send.at[2], recv.at[2 + c],
+                      r * TILE_COLS + beside()))
 
     def each_edge(action):
         action(col_copy(0, r, east))
@@ -302,6 +337,33 @@
 
     for k in range(1, TILE_COLS):
         arrived(2 + (c + k) % TILE_COLS)
+
+    spare = got.shape[0] // 4
+    inner = got.shape[0] - 2 * spare
+
+    def enter(i):
+        values = gather_row(got, spare + i, c, halo)
+        held[i] = values
+        part[0, i] = convolve(values, regc[0], regw[0])
+
+    def update(k, i):
+        return add_rows(held[i], part[k, i - 1], part[k, i], part[k, i + 1], regc[2 * k + 1])
+
+    def follow(k, i):
+        values = update(k - 1, i).astype(F32)
+        held[i] = values
+        part[k, i] = convolve(values, regc[2 * k], regw[k])
+
+    lag = 3
+    for i in range(inner + lag * blocks):
+        if i < inner:
+            enter(i)
+        for k in range(1, blocks):
+            if k <= i - lag * k < inner - k:
+                follow(k, i - lag * k)
+        row = i - lag * blocks
+        if blocks <= row < inner - blocks:
+            field[row - blocks] = update(blocks - 1, row)
 
     @pl.when(north)
     def _():
@@ -368,9 +430,12 @@
             shape((cw, 3 * fl), BF16),
             shape((9, 128, 128), BF16),
             shape((cw, 128), BF16),
+            shape((lines_n - 2 * (lines_n // 4), cin, cw), F32),
+            shape((blocks, lines_n - 2 * (lines_n // 4), 3 * cin, cw), F32),
+            shape((lines_n - 2 * (lines_n // 4) - 2 * blocks, cin, cw), BF16),
         ),
         in_specs=[hbm] * 10,
-        out_specs=(vmem,) * 12,
+        out_specs=(vmem,) * 15,
         scratch_shapes=[
             pltpu.VMEM((cin, band_rows, clon), BF16),
             pltpu.VMEM((TILE_COLS, band_rows, cin + 16, 128), BF16),
@@ -387,24 +452,22 @@
             dma((2 * TILE_COLS,)), dma((8,)), dma((10,)), dma((10,)), dma((11,)),
         ],
         compiler_params=pltpu.CompilerParams(
-            collective_id=0, has_side_effects=True, vmem_limit_bytes=20_000_000),
+            collective_id=0, has_side_effects=True, vmem_limit_bytes=24_000_000),
     )(*[pltpu.with_memory_space_constraint(x, pltpu.HBM) for x in (
         coarse, noisy, gain, regb, regs, liftb, midg, midb, lifts, mids)])
 
 
 def tile_kernel(
-    dims, got, got_cols, own_cols, grid, regw, regc, liftw, gains, midw, lon, sidew, chosen, out,
+    dims, got, got_cols, own_cols, grid, regw, regc, liftw, gains, midw, lon, sidew, chosen, held_in, part_in, field_in, out,
     held, part, field, lines, upper, sides, bands, unit, raw, prod, edges, rows_out, stage, sems,
 ):
     cin, ch, nout, fr, fl = dims
     lines_n, count, cw = got.shape[0], field.shape[0], field.shape[2]
     blocks = regw.shape[0]
     halo = blocks + 1
-    span = 2 * halo * TILE_COLS
     me = lax.axis_index("lat")
     tile_row, tile_rows = me // TILE_COLS, lax.axis_size("lat") // TILE_COLS
     c = me % TILE_COLS
-    after_seam = (c + 1) % TILE_COLS
     top, bottom = tile_row == 0, tile_row == tile_rows - 1
     steps = bands.shape[0]
     wide = fl // 128
@@ -419,34 +482,26 @@
             return jnp.where(bottom, 0.0, values)
         return values
 
-    def spread(k, i, values):
-        values = activate(values, regc[2 * k][:, :1])
-        taps = jnp.concatenate(
-            [pltpu.roll(values, 1, 1).astype(BF16), values.astype(BF16), pltpu.roll(values, cw - 1, 1).astype(BF16)],
-            axis=0)
-        part[k % 2, i] = jnp.dot(regw[k], taps, preferred_element_type=F32)
+    def ready(k, i):
+        return spare + k <= i < lines_n - spare - k
+
+    def product(k, i):
+        return part_in[k, i - spare] if ready(k, i) else part[k % 2, i]
 
     def enter(i):
-        side = got[i, cin:, :].astype(F32)
-        outer = []
-        for g in range(cin // 16):
-            after = pltpu.roll(side, 128 - halo - g * span - 2 * halo * after_seam, 1)
-            before = pltpu.roll(side, 128 - halo - g * span - 2 * halo * c, 1)
-            outer.append(jnp.where(lane < halo, after, jnp.where(lane >= 128 - halo, before, 0.0)))
-        values = jnp.concatenate([got[i, :cin, :].astype(F32), jnp.concatenate(outer, axis=0)], axis=1)
-        values = known(i, values)
+        values = known(i, gather_row(got, i, c, halo))
         held[i] = values
-        spread(0, i, values)
+        part[0, i] = convolve(values, regc[0], regw[0])
 
     def update(k, i):
-        values = held[i] + part[k % 2, i - 1, :cin, :] + part[k % 2, i, cin:2 * cin, :] + part[k % 2, i + 1, 2 * cin:, :]
-        values = (values + regc[2 * k + 1][:, :1]).astype(BF16)
+        values = held_in[i - spare] if ready(k, i) else held[i]
+        values = add_rows(values, product(k, i - 1), product(k, i), product(k, i + 1), regc[2 * k + 1])
         return known(i, values.astype(F32))
 
     def follow(k, i):
         values = update(k - 1, i)
         held[i] = values
-        spread(k, i, values)
+        part[k % 2, i] = convolve(values, regc[2 * k], regw[k])
 
     def widen(first, last):
         coarse = field[first:last].reshape((last - first) * cin, cw)
@@ -591,23 +646,23 @@
     def settle(row):
         field[row - halo] = update(blocks - 1, row).astype(BF16)
 
+    def spread(lines_at):
+        widen(*lines_at)
+
+    held_lines = lines_n - 2 * spare - 2 * blocks
+    low = spare + blocks - halo
+    for n in range(held_lines):
+        field[low + n] = field_in[n]
     plan = []
-    lag = 3
-    for i in range(1, lines_n - 1 + lag * blocks):
-        if i < lines_n - 1:
-            plan.append((enter, i))
-        for k in range(1, blocks):
-            row = i - lag * k
-            if 1 + k <= row < lines_n - 1 - k:
-                plan.append((functools.partial(follow, k), row))
-        row = i - lag * blocks
-        if halo <= row < lines_n - halo:
-            plan.append((settle, row))
-            line = row - halo
-            if line % 2:
-                plan.append((lambda n: widen(n - 1, n + 1), line))
-            elif line == count - 1:
-                plan.append((lambda n: widen(n, n + 1), line))
+    for k in range(blocks):
+        for i in range(1 + k, lines_n - 1 - k):
+            if not ready(k, i):
+                plan.append((functools.partial(follow, k) if k else enter, i))
+        if k == 0:
+            plan.insert(3, (spread, (low, low + held_lines // 2)))
+            plan.append((spread, (low + held_lines // 2, low + held_lines)))
+    plan += [(settle, i) for i in range(halo, spare + blocks)] + [(spread, (0, low))]
+    plan += [(settle, i) for i in range(lines_n - spare - blocks, lines_n - halo)] + [(spread, (low + held_lines, count))]
     plan += [(lambda _: edge_pick(), 0), (raised, 0), (raised, 1), (lambda _: edge_pack(), 0), (raised, 2),
              (lifted, 0), (raised, 3), (edge_blend, 0), (edge_blend, 1), (edge_blend, 2), (raised, 4), (lifted, 1), (raised, 5),
              (lambda _: edge_lift(), 0), (lifted, 2), (raised, 6), (lambda _: edge_finish(), 0), (lifted, 3), (finished, 0),
@@ -624,10 +679,10 @@
         for o in range(share_out):
             shrink(n + 1, shrink_at + o)
         emit(n, (i % halves) * steps + u, u)
+        if last is None or last + 4 < fr + 2:
+            finish(e + 4, (u + 4) % steps)
         if last is None or last + 1 < fr:
             mid((u + 1) % steps)
-        if last is None or last + 4 < fr + 2:
-            finish(e + 4, (u + 4) % steps)
         if last is None or last + 5 < fr + 2:
             lift((u + 5) % steps, u + 5)
         if last is None:
@@ -661,11 +716,18 @@
     groups = fr // group
     if groups >= 3:
         flushed(groups - 3).wait()
-    for o in range(blocks_out):
-        shrink(groups - 1, o)
-    flushed(groups - 1).start()
-    for n in range(max(groups - 2, 0), groups):
-        flushed(n).wait()
+    last = groups - 1
+    parts = [pltpu.make_async_copy(
+        stage.at[last % 2, pl.ds(h * ch // 2, ch // 2)],
+        out.at[0, pl.ds(h * ch // 2, ch // 2), pl.ds(last * group, group), :], sems.at[2 + h]) for h in range(2)]
+    for h in range(2):
+        for o in range(blocks_out // 2):
+            shrink(last, h * (blocks_out // 2) + o)
+        parts[h].start()
+    if groups >= 2:
+        flushed(groups - 2).wait()
+    for copy in parts:
+        copy.wait()
 
 
 def tile_program(dims, prepared):
@@ -698,7 +760,7 @@
             pltpu.VMEM((ch, 128), BF16),
             pltpu.VMEM((2, fl // 128, ch * group, 128), F32),
             pltpu.VMEM((2, ch, group, fl), BF16),
-            pltpu.SemaphoreType.DMA((2,)),
+            pltpu.SemaphoreType.DMA((4,)),
         ],
         compiler_params=pltpu.CompilerParams(vmem_limit_bytes=44_000_000),
     )(*prepared)

time: 38.2 us -> 37 us (0.969)
  Pallas kernels: 38.1 us -> 36.9 us
    pallas_call x1, Pallas kernels: 27.4 us -> 26.2 us  [tile_program(): pl.pallas_call(functools.partial(tile_kernel, dims), out_shape=jax.ShapeD...]
where the time goes in v4:
time: 37 us; the launch traced here: 36.9 us
  Pallas kernels  36.9 us (100%)
    pallas_call x1, Pallas kernels, tile_program(): pl.pallas_call(functools.partial(tile_kernel, dims), out_shape=jax.ShapeD...  26.2 us
    pallas_call x1, Pallas kernels, first_program(): pl.pallas_call(first_kernel, out_shape=(shape((lines_n, cin + 16, 128), B...  10.7 us

profile of v4, /device:TPU:0, one launch (start us, length us, event | category | flops | bytes accessed | tf_op | source)
XLA Modules:
  0.0 36.9 jit_solution(2463162028747420286)
XLA Ops:
  0.0 10.7 %shard_map.100 = (bf16[16,96,128]{2,1,0:T(8,128)(2,1)S(1)}, bf16[8,16,128]{2,1,0:T(8,128)(2,1)S(1)}, bf16[16,128]{1,0:T(8,128)(2,1)S(1)}, f32[4,144,128]{2,1,0:T...) custom-call(bf16[80,2,512]{2,1,0:T(2,128)(2,1)} %coarse.1, ...), custom_call_target="tpu_custom_call" | custom-call | tf_op jit(solution)/shard_map/pallas_call | solution.py:418
  10.7 26.2 %shard_map.101 = bf16[1,192,32,512]{3,2,1,0:T(8,128)(2,1)} custom-call(bf16[16,96,128]{2,1,0:T(8,128)(2,1)S(1)} %get-tuple-element.20.got, bf16[8,16,128]{2,1,0:T(8,128)(2,1)S(1)} %get-tuple-element.21.got_cols, bf16[16,128]{1,0:T(8,128)(2,1)S(1)} %get-tuple-element.22.own_cols, f32[4,144,128]{2,1,0:T(8,128)S(1)} %get-tuple-element.23.grid, ...), custom_call_target="tpu_custom_call" | custom-call | tf_op jit(solution)/shard_map/pallas_call | solution.py:744

commit v5 on v4

--- a/solution.py
+++ b/solution.py
@@ -163,10 +163,9 @@
             pieces[b, sub, cin:, :] = side.astype(BF16)
 
     loads[1].wait()
-    ends = []
-    for n in range(nout):
-        ends += [tile[n, :2, :].astype(F32), tile[n, fr - 2:, :].astype(F32)]
-    rows[...] = jnp.concatenate(ends, axis=0).astype(BF16)
+    for side, first in ((0, 0), (1, fr - 2)):
+        lines = jnp.concatenate([tile[n, first:first + 2, :].astype(F32) for n in range(nout)], axis=0)
+        rows[side] = jnp.concatenate([lines[:, :fl // 2], lines[:, fl // 2:]], axis=0).astype(BF16)
     pick_row = lax.broadcasted_iota(jnp.int32, (4 * nout, 128), 0)
     pick_lane = lax.broadcasted_iota(jnp.int32, (4 * nout, 128), 1)
     packed = jnp.zeros((4 * nout, fr), F32)
@@ -209,7 +208,7 @@
         return remote(cols, got_cols.at[slot], nsend.at[slot], nrecv.at[slot], row * TILE_COLS + col)
 
     def row_copy(slot, row):
-        return remote(rows, far_rows.at[slot], nsend.at[8 + slot], nrecv.at[8 + slot], row * TILE_COLS + c)
+        return remote(rows.at[1 - slot], far_rows.at[slot], nsend.at[8 + slot], nrecv.at[8 + slot], row * TILE_COLS + c)
 
     def each_band(action):
         for col, side, row, slot, span_rows in (
@@ -247,13 +246,13 @@
     each_band(lambda copy: copy.start())
     own = pltpu.make_async_copy(pieces.at[c], landing(2 + c, whole), local.at[5])
     own.start()
+    each_edge(lambda copy: copy.start())
 
     loads[2].wait()
     for k in range(blocks):
         for p in range(3):
             for q in range(3):
                 regw[k, p * cin:(p + 1) * cin, q * cin:(q + 1) * cin] = regv[9 * k + 3 * p + q]
-    each_edge(lambda copy: copy.start())
 
     loads[3].wait()
     for tap in range(9):
@@ -276,12 +275,10 @@
     eye = jnp.where(lax.broadcasted_iota(jnp.int32, (ch, ch), 0) == lax.broadcasted_iota(jnp.int32, (ch, ch), 1), 1.0, 0.0)
     liftw[...] = nt_dot(eye.astype(BF16), liftt[...]).astype(BF16)
 
-    position = lax.broadcasted_iota(jnp.int32, (1, 3 * fl), 1)
-    shift = jnp.where(position >= 2 * fl, 2, jnp.where(position >= fl, 1, 0))
-    low, weight = lon_split(position - shift * fl + shift - 1)
+    low, weight = lon_split(lax.broadcasted_iota(jnp.int32, (1, fl), 1))
     low_lane = jnp.where(low < 0, low + cw, low)
     high_lane = jnp.where(low + 1 < 0, low + 1 + cw, low + 1)
-    coarse_lane = lax.broadcasted_iota(jnp.int32, (cw, 3 * fl), 0)
+    coarse_lane = lax.broadcasted_iota(jnp.int32, (cw, fl), 0)
     lon[...] = jnp.where(coarse_lane == low_lane, 1.0 - weight,
                          jnp.where(coarse_lane == high_lane, weight, 0.0)).astype(BF16)
 
@@ -333,7 +330,7 @@
         if slot < 8:
             remote(cols, got_cols.at[slot], nsend.at[slot], nrecv.at[slot], me).wait_recv()
         else:
-            remote(rows, far_rows.at[slot - 8], nsend.at[slot], nrecv.at[slot], me).wait_recv()
+            remote(rows.at[0], far_rows.at[slot - 8], nsend.at[slot], nrecv.at[slot], me).wait_recv()
 
     for k in range(1, TILE_COLS):
         arrived(2 + (c + k) % TILE_COLS)
@@ -390,9 +387,10 @@
 
     for n in range(nout):
         for j in range(wide):
-            at = slice(j * 128, (j + 1) * 128)
-            above = far_rows[0, :, at].astype(F32)[4 * n + 2:4 * n + 4]
-            below = far_rows[1, :, at].astype(F32)[4 * n:4 * n + 2]
+            at = slice(j * 128 % (fl // 2), j * 128 % (fl // 2) + 128)
+            row = 2 * n + 2 * nout * (j * 128 // (fl // 2))
+            above = far_rows[0, :, at].astype(F32)[row:row + 2]
+            below = far_rows[1, :, at].astype(F32)[row:row + 2]
             grid[j, n * tall:n * tall + 2, :] = jnp.where(top, 0.0, above)
             grid[j, n * tall + 2 + fr:(n + 1) * tall, :] = jnp.where(bottom, 0.0, below)
 
@@ -427,7 +425,7 @@
             shape((ch, 3 * slab), BF16),
             shape((ch, 128), F32),
             shape((ch, 9 * ch + 16), BF16),
-            shape((cw, 3 * fl), BF16),
+            shape((cw, fl), BF16),
             shape((9, 128, 128), BF16),
             shape((cw, 128), BF16),
             shape((lines_n - 2 * (lines_n // 4), cin, cw), F32),
@@ -440,8 +438,8 @@
             pltpu.VMEM((cin, band_rows, clon), BF16),
             pltpu.VMEM((TILE_COLS, band_rows, cin + 16, 128), BF16),
             pltpu.VMEM((nout, fr, fl), BF16),
-            pltpu.VMEM((4 * nout, fl), BF16),
-            pltpu.VMEM((2, 4 * nout, fl), BF16),
+            pltpu.VMEM((2, 4 * nout, fl // 2), BF16),
+            pltpu.VMEM((2, 4 * nout, fl // 2), BF16),
             pltpu.VMEM(gain.shape, F32),
             pltpu.VMEM(regb.shape, F32),
             pltpu.VMEM((3, 1, ch), F32),
@@ -505,9 +503,14 @@
 
     def widen(first, last):
         coarse = field[first:last].reshape((last - first) * cin, cw)
-        for q in range(3):
-            lines[first:last, q * cin:(q + 1) * cin, :] = jnp.dot(
-                coarse, lon[:, q * fl:(q + 1) * fl], preferred_element_type=F32).reshape(last - first, cin, fl)
+        lines[first:last] = jnp.dot(coarse, lon[...], preferred_element_type=F32).reshape(last - first, cin, fl)
+
+    def neighbours(values, seam_l, seam_r):
+        parts = [values[:, j * 128:(j + 1) * 128] for j in range(wide)]
+        onward = [seam_l] + [pltpu.roll(v, 1, 1) for v in parts]
+        back = [pltpu.roll(v, 127, 1) for v in parts] + [seam_r]
+        return (jnp.concatenate([jnp.where(lane_first, onward[j], onward[j + 1]) for j in range(wide)], axis=1),
+                jnp.concatenate([jnp.where(lane_last, back[j + 1], back[j]) for j in range(wide)], axis=1))
 
     def blend(t):
         return lat_split(t, top, bottom, count, tile_row * fr, fr * tile_rows)
@@ -550,8 +553,16 @@
         a, b, share, ok = blend(jnp.int32(t))
         wa = jnp.where(ok, 1.0 - share, 0.0)
         wb = jnp.where(ok, share, 0.0)
-        for o in range(0, 3 * cin, 16):
-            upper[slot, o:o + 16, :] = (wa * lines[a, o:o + 16, :] + wb * lines[b, o:o + 16, :]).astype(BF16)
+        static = isinstance(t, int)
+        for o in range(0, cin, 16):
+            values = (wa * lines[a, o:o + 16, :] + wb * lines[b, o:o + 16, :]).astype(BF16)
+            seam = sides[cin + o:cin + o + 16, :]
+            seam_l = pltpu.roll(seam, (128 - t) % 128 if static else 128 - t, 1)
+            seam_r = pltpu.roll(seam, (127 + HALF - t) % 128 if static else 127 + HALF - t, 1)
+            onward, back = neighbours(values, seam_l, seam_r)
+            upper[slot, o:o + 16, :] = onward
+            upper[slot, cin + o:cin + o + 16, :] = values
+            upper[slot, 2 * cin + o:2 * cin + o + 16, :] = back
         upper[slot, 3 * cin:slab, :] = noise_rows(t)
 
     edge_row = jnp.where(lane < HALF, lane, lane - HALF)
@@ -598,16 +609,12 @@
             half = raw[slot, o:o + 16, :] * inverse * half_gain
             values = (half + half * jnp.tanh(half)).astype(BF16)
             edge = edges[o:o + 16, :]
-            parts = [values[:, j * 128:(j + 1) * 128] for j in range(wide)]
-            onward = [pltpu.roll(v, 1, 1) for v in parts]
-            back = [pltpu.roll(v, 127, 1) for v in parts]
             edge_l = pltpu.roll(edge, 128 - l, 1)
-            edge_r = pltpu.roll(edge, 128 + HALF - 1 - l, 1)
+            edge_r = pltpu.roll(edge, 127 + HALF - l, 1)
+            onward, back = neighbours(values, edge_l, edge_r)
+            bands[slot, o:o + 16, :] = onward
             bands[slot, ch + o:ch + o + 16, :] = values
-            bands[slot, o:o + 16, :] = jnp.concatenate(
-                [jnp.where(lane_first, onward[j - 1] if j else edge_l, onward[j]) for j in range(wide)], axis=1)
-            bands[slot, 2 * ch + o:2 * ch + o + 16, :] = jnp.concatenate(
-                [jnp.where(lane_last, back[j + 1] if j < wide - 1 else edge_r, back[j]) for j in range(wide)], axis=1)
+            bands[slot, 2 * ch + o:2 * ch + o + 16, :] = back
 
     def mid(slot):
         window = jnp.concatenate([bands[(slot + n) % steps] for n in range(3)] + [unit[...]], axis=0)
@@ -618,11 +625,11 @@
 
     def flushed(n):
         return pltpu.make_async_copy(
-            stage.at[n % 2], out.at[0, :, pl.ds(pl.multiple_of(n * group, group), group), :], sems.at[n % 2])
-
-    def shrink(n, o):
-        for j in range(wide):
-            block = rows_out[n % 2, j, pl.ds(pl.multiple_of(o * 8 * group, 8 * group), 8 * group), :]
+            stage.at[n % 2], out.at[0, :, pl.ds(n * group if isinstance(n, int) else pl.multiple_of(n * group, group), group), :], sems.at[n % 2])
+
+    def shrink(n, o, only=None):
+        for j in range(wide) if only is None else (only,):
+            block = rows_out[n % 2, j, pl.ds(o * 8 * group if isinstance(o, int) else pl.multiple_of(o * 8 * group, 8 * group), 8 * group), :]
             stage[n % 2, pl.ds(o * 8, 8), :, j * 128:(j + 1) * 128] = block.reshape(8, group, 128).astype(BF16)
 
     def emit(n, spot, slot):
@@ -663,10 +670,10 @@
             plan.append((spread, (low + held_lines // 2, low + held_lines)))
     plan += [(settle, i) for i in range(halo, spare + blocks)] + [(spread, (0, low))]
     plan += [(settle, i) for i in range(lines_n - spare - blocks, lines_n - halo)] + [(spread, (low + held_lines, count))]
-    plan += [(lambda _: edge_pick(), 0), (raised, 0), (raised, 1), (lambda _: edge_pack(), 0), (raised, 2),
-             (lifted, 0), (raised, 3), (edge_blend, 0), (edge_blend, 1), (edge_blend, 2), (raised, 4), (lifted, 1), (raised, 5),
-             (lambda _: edge_lift(), 0), (lifted, 2), (raised, 6), (lambda _: edge_finish(), 0), (lifted, 3), (finished, 0),
-             (raised, 7), (finished, 1), (lifted, 4), (finished, 2), (mid, 0), (finished, 3)]
+    plan += [(lambda _: edge_pick(), 0), (lambda _: edge_pack(), 0), (edge_blend, 0), (raised, 0), (edge_blend, 1), (raised, 1),
+             (edge_blend, 2), (raised, 2), (lifted, 0), (raised, 3), (lambda _: edge_lift(), 0), (lifted, 1), (raised, 4),
+             (lifted, 2), (raised, 5), (lambda _: edge_finish(), 0), (lifted, 3), (raised, 6), (finished, 0),
+             (lifted, 4), (raised, 7), (finished, 1), (finished, 2), (mid, 0), (finished, 3)]
     for action, n in plan:
         action(n)
 
@@ -676,17 +683,17 @@
     def step(i, u, e, last):
         n = i // halves
         shrink_at = (i % halves) * (blocks_out // halves) + u * share_out
+        emit(n, (i % halves) * steps + u, u)
         for o in range(share_out):
             shrink(n + 1, shrink_at + o)
-        emit(n, (i % halves) * steps + u, u)
+        if last is None:
+            raise_row(e + 8, u)
         if last is None or last + 4 < fr + 2:
             finish(e + 4, (u + 4) % steps)
         if last is None or last + 1 < fr:
             mid((u + 1) % steps)
         if last is None or last + 5 < fr + 2:
             lift((u + 5) % steps, u + 5)
-        if last is None:
-            raise_row(e + 8, u)
 
     trips = fr // steps
 
@@ -708,22 +715,21 @@
         return 0
 
     lax.fori_loop(0, trips - 1, trip, 0)
-    i = jnp.int32(trips - 1)
-    begin(i)
-    for u in range(steps):
-        step(i, u, i * steps + u, fr - steps + u)
-    finish_trip(i)
     groups = fr // group
+    last = groups - 1
     if groups >= 3:
         flushed(groups - 3).wait()
-    last = groups - 1
+    for u in range(steps):
+        step(trips - 1, u, (trips - 1) * steps + u, fr - steps + u)
+    if groups >= 2:
+        flushed(groups - 2).start()
     parts = [pltpu.make_async_copy(
-        stage.at[last % 2, pl.ds(h * ch // 2, ch // 2)],
-        out.at[0, pl.ds(h * ch // 2, ch // 2), pl.ds(last * group, group), :], sems.at[2 + h]) for h in range(2)]
-    for h in range(2):
-        for o in range(blocks_out // 2):
-            shrink(last, h * (blocks_out // 2) + o)
-        parts[h].start()
+        stage.at[last % 2, :, :, pl.ds(j * 128, 128)],
+        out.at[0, :, pl.ds(last * group, group), pl.ds(j * 128, 128)], sems.at[2 + j]) for j in range(wide)]
+    for j in range(wide):
+        for o in range(blocks_out):
+            shrink(last, o, j)
+        parts[j].start()
     if groups >= 2:
         flushed(groups - 2).wait()
     for copy in parts:
@@ -750,7 +756,7 @@
             pltpu.VMEM((lines_n, cin, cw), F32),
             pltpu.VMEM((2, lines_n, 3 * cin, cw), F32),
             pltpu.VMEM((count, cin, cw), BF16),
-            pltpu.VMEM((count, 3 * cin, fl), F32),
+            pltpu.VMEM((count, cin, fl), F32),
             pltpu.VMEM((steps, slab, fl), BF16),
             pltpu.VMEM((3 * slab, 128), BF16),
             pltpu.VMEM((steps, 3 * ch, fl), BF16),
@@ -760,7 +766,7 @@
             pltpu.VMEM((ch, 128), BF16),
             pltpu.VMEM((2, fl // 128, ch * group, 128), F32),
             pltpu.VMEM((2, ch, group, fl), BF16),
-            pltpu.SemaphoreType.DMA((4,)),
+            pltpu.SemaphoreType.DMA((2 + fl // 128,)),
         ],
         compiler_params=pltpu.CompilerParams(vmem_limit_bytes=44_000_000),
     )(*prepared)

time: 37 us -> 36.8 us (level)
  no operation moved by 1% of the time
where the time goes in v5:
time: 36.8 us; the launch traced here: 36.7 us
  Pallas kernels  36.7 us (100%)
    pallas_call x1, Pallas kernels, tile_program(): pl.pallas_call(functools.partial(tile_kernel, dims), out_shape=jax.ShapeD...  26.2 us
    pallas_call x1, Pallas kernels, first_program(): pl.pallas_call(first_kernel, out_shape=(shape((lines_n, cin + 16, 128), B...  10.5 us

profile of v5, /device:TPU:0, one launch (start us, length us, event | category | flops | bytes accessed | tf_op | source)
XLA Modules:
  0.0 36.7 jit_solution(3688504508210514054)
XLA Ops:
  0.0 10.5 %shard_map.100 = (bf16[16,96,128]{2,1,0:T(8,128)(2,1)S(1)}, bf16[8,16,128]{2,1,0:T(8,128)(2,1)S(1)}, bf16[16,128]{1,0:T(8,128)(2,1)S(1)}, f32[4,144,128]{2,1,0:T...) custom-call(bf16[80,2,512]{2,1,0:T(2,128)(2,1)} %coarse.1, ...), custom_call_target="tpu_custom_call" | custom-call | tf_op jit(solution)/shard_map/pallas_call | solution.py:416
  10.5 26.2 %shard_map.101 = bf16[1,192,32,512]{3,2,1,0:T(8,128)(2,1)} custom-call(bf16[16,96,128]{2,1,0:T(8,128)(2,1)S(1)} %get-tuple-element.20.got, bf16[8,16,128]{2,1,0:T(8,128)(2,1)S(1)} %get-tuple-element.21.got_cols, bf16[16,128]{1,0:T(8,128)(2,1)S(1)} %get-tuple-element.22.own_cols, f32[4,144,128]{2,1,0:T(8,128)S(1)} %get-tuple-element.23.grid, ...), custom_call_target="tpu_custom_call" | custom-call | tf_op jit(solution)/shard_map/pallas_call | solution.py:750
